TPU v7x, 512 devices: a whole 4x4x16 slice. The times are simulated.
512 devices in a mesh: plane: 8 (over x, core), span: 16 (over z), height: 4 (over y).
Axes of the slice: x: 4, y: 4, z: 16, core: 2. Of those that a mesh axis runs over, the one named last changes fastest.
Arguments:
- noisy: bfloat16 [8, 3, 256, 2048], P('plane', None, 'height', 'span'), may hold values from -6 to 6
- coarse_cond: bfloat16 [512, 8, 3, 32, 256], P(('plane', 'span', 'height')), may hold values from -6 to 6
- timestep: int32 [1], replicated, may hold values from 20 to 899
- owner: int32 [1], replicated, may hold values from 0 to 511
- w_embed: float32 [64, 256], replicated, may hold values from -0.75 to 0.75
- w_biases: float32 [256, 448], replicated, may hold values from -0.375 to 0.375
- w_enter: bfloat16 [3, 64, 18], replicated, may hold values from -1.5 to 1.5
- pool_fine: bfloat16 [4, 128, 64], replicated, may hold values from -0.5 to 0.5
- pool_mid: bfloat16 [4, 256, 128], replicated, may hold values from -0.375 to 0.375
- w_squeeze: bfloat16 [128, 256], replicated, may hold values from -0.375 to 0.375
- w_across: bfloat16 [3, 256, 128], replicated, may hold values from -0.5 to 0.5
- w_middle: bfloat16 [3, 256, 768], replicated, may hold values from -0.21875 to 0.21875
- rise_mid: bfloat16 [4, 128, 256], replicated, may hold values from -0.5 to 0.5
- decode_mid: bfloat16 [3, 128, 384], replicated, may hold values from -0.3125 to 0.3125
- rise_fine: bfloat16 [4, 64, 128], replicated, may hold values from -0.75 to 0.75
- decode_fine: bfloat16 [3, 64, 192], replicated, may hold values from -0.4375 to 0.4375
- w_leave: bfloat16 [3, 3, 192], replicated, may hold values from -0.4375 to 0.4375
Outputs:
- noise_pred: bfloat16 [8, 3, 256, 2048], P('plane', None, 'height', 'span')
- next_sample: float32 [8, 3, 256, 2048], P('plane', None, 'height', 'span')
Inputs may be any that keep to these rules, and one draw needn't show every extreme that they name: The timestep lies in the plan's range and is at least 20. The owner is a device index in the mesh order plane, span, height.
All inputs are finite; a program needn't handle non-finite values.
Results may differ from a plain program's by a relative error of at most 0.03.
Values may be sent and summed in bfloat16 or wider, within the bound.
A program may use at most 64 MiB of HBM per device.

v0:
```python
import math

import jax
import jax.numpy as jnp
from jax import lax
from jax.sharding import PartitionSpec as P

CF = 8
TSTEPS = 1000
STRIDE = 20


def with_halo(block, sides, width):
    for axis, dim in sides:
        count = lax.axis_size(axis)
        forward = [(i, i + 1) for i in range(count - 1)]
        backward = [(target, source) for source, target in forward]
        low = lax.ppermute(
            lax.slice_in_dim(block, block.shape[dim] - width, None, axis=dim), axis, forward
        )
        high = lax.ppermute(lax.slice_in_dim(block, 0, width, axis=dim), axis, backward)
        block = jnp.concatenate([low, block, high], axis=dim)
    return block


def spread_2(array, axis, root):
    mine = lax.axis_index(axis) == root
    return lax.psum(jnp.where(mine, array, jnp.zeros_like(array)), axis)


def stencil(padded, weight, rows, cols):
    total = None
    for lift in range(3):
        stacked = jnp.concatenate(
            [padded[:, lift : lift + rows, step : step + cols] for step in range(3)], axis=0
        )
        term = jnp.einsum("ok,khs->ohs", weight[lift], stacked, preferred_element_type=jnp.float32)
        total = term if total is None else total + term
    return total


def widen(field):
    return with_halo(field, (("span", 2), ("height", 1)), 1)


def pooled(field, weight):
    chans, rows, cols = field.shape
    outs = weight.shape[1]
    grid = field.reshape(chans, rows // 2, 2, cols // 2, 2)
    kernel = weight.reshape(2, 2, outs, chans)
    return jnp.einsum("aboc,cxayb->oxy", kernel, grid, preferred_element_type=jnp.float32)


def raised(field, weight):
    chans, rows, cols = field.shape
    outs = weight.shape[1]
    kernel = weight.reshape(2, 2, outs, chans)
    spread = jnp.einsum("aboc,cxy->oxayb", kernel, field, preferred_element_type=jnp.float32)
    return spread.reshape(outs, 2 * rows, 2 * cols)


def plan(stepnum):
    phase = (stepnum.astype(jnp.float32) / TSTEPS + 0.008) / 1.008 * (math.pi / 2.0)
    return jnp.cos(phase) ** 2


def time_bias(timestep, w_embed, w_biases):
    half = w_embed.shape[0] // 2
    freqs = jnp.exp(-math.log(10000.0) * jnp.arange(half, dtype=jnp.float32) / half)
    angles = timestep[0].astype(jnp.float32) * freqs
    waves = jnp.concatenate([jnp.sin(angles), jnp.cos(angles)])
    hidden = jax.nn.silu(jnp.dot(waves, w_embed, precision=lax.Precision.HIGHEST))
    return jnp.dot(hidden, w_biases, precision=lax.Precision.HIGHEST)


def shards(
    noisy,
    coarse_cond,
    timestep,
    owner,
    w_embed,
    w_biases,
    w_enter,
    pool_fine,
    pool_mid,
    w_squeeze,
    w_across,
    w_middle,
    rise_mid,
    decode_mid,
    rise_fine,
    decode_fine,
    w_leave,
):
    sample = noisy[0]
    rows, cols = (sample.shape[1], sample.shape[2])
    biases = time_bias(timestep, w_embed, w_biases)
    first = w_enter.shape[1]
    second = pool_fine.shape[1]
    bias_one = biases[:first][:, None, None]
    bias_two = biases[first : first + second][:, None, None]
    bias_three = biases[first + second :][:, None, None]
    slot = coarse_cond[0]
    plane_index = lax.axis_index("plane")
    coarse_rows = rows // CF
    coarse_cols = cols // CF
    full = spread_2(slot, ("plane", "span", "height"), owner[0])
    local_cond = lax.dynamic_index_in_dim(full, plane_index, 0, keepdims=False)
    start_row = lax.axis_index("height") * coarse_rows
    start_col = lax.axis_index("span") * coarse_cols
    patch = lax.dynamic_slice(
        local_cond, (jnp.int32(0), start_row, start_col), (3, coarse_rows, coarse_cols)
    )
    lifted = jnp.repeat(jnp.repeat(patch, CF, axis=1), CF, axis=2)
    entry = jnp.concatenate([sample, lifted], axis=0)
    level_one = jax.nn.silu(stencil(widen(entry), w_enter, rows, cols) + bias_one).astype(
        jnp.bfloat16
    )
    level_two = jax.nn.silu(pooled(level_one, pool_fine) + bias_two).astype(jnp.bfloat16)
    level_three = jax.nn.silu(pooled(level_two, pool_mid) + bias_three).astype(jnp.bfloat16)
    squeezed = jnp.einsum(
        "ic,chs->ihs", w_squeeze, level_three, preferred_element_type=jnp.float32
    ).astype(jnp.bfloat16)
    beside_all = with_halo(squeezed[None], (("plane", 0),), 1)
    mixed = level_three.astype(jnp.float32)
    for tap in range(3):
        mixed = mixed + jnp.einsum(
            "oi,ihs->ohs", w_across[tap], beside_all[tap], preferred_element_type=jnp.float32
        )
    mixed = mixed.astype(jnp.bfloat16)
    coarse = jax.nn.silu(stencil(widen(mixed), w_middle, rows // 4, cols // 4)).astype(jnp.bfloat16)
    joined_two = (raised(coarse, rise_mid) + level_two.astype(jnp.float32)).astype(jnp.bfloat16)
    decoded_two = jax.nn.silu(stencil(widen(joined_two), decode_mid, rows // 2, cols // 2)).astype(
        jnp.bfloat16
    )
    joined_one = (raised(decoded_two, rise_fine) + level_one.astype(jnp.float32)).astype(
        jnp.bfloat16
    )
    decoded_one = jax.nn.silu(stencil(widen(joined_one), decode_fine, rows, cols)).astype(
        jnp.bfloat16
    )
    guess = stencil(widen(decoded_one), w_leave, rows, cols)
    noise_pred = guess.astype(jnp.bfloat16)
    now = plan(timestep[0])
    prior = plan(timestep[0] - STRIDE)
    sample_f = sample.astype(jnp.float32)
    guess_f = noise_pred.astype(jnp.float32)
    clean = (sample_f - jnp.sqrt(1.0 - now) * guess_f) / jnp.sqrt(now)
    next_sample = jnp.sqrt(prior) * clean + jnp.sqrt(1.0 - prior) * guess_f
    return (noise_pred[None], next_sample[None])


def solution(mesh):
    in_specs = (
        P("plane", None, "height", "span"),
        P(("plane", "span", "height"), None, None, None, None),
        P(),
        P(),
        P(),
        P(),
        P(),
        P(),
        P(),
        P(),
        P(),
        P(),
        P(),
        P(),
        P(),
        P(),
        P(),
    )
    out_specs = (P("plane", None, "height", "span"), P("plane", None, "height", "span"))
    return jax.shard_map(shards, mesh=mesh, in_specs=in_specs, out_specs=out_specs, check_vma=False)
```

profile of v0, /device:TPU:66, one launch (start us, length us, event | category | flops | bytes accessed | tf_op | source)
XLA Modules:
  0.0 656.4 jit_solution(9261989726697439908)
XLA Ops:
  11.4 467.3 %all-reduce.2.cloned.1.call-done = bf16[8,3,32,256]{3,2,1,0:T(8,128)(2,1)} async-done(((bf16[8,3,32,256]{3,2,1,0:T(8,128)(2,1)}), bf16[8,3,32,256]{3,2,1,0:T(8,128)(2,1)}) %all-reduce.2.cloned.1.call-update) | async-done | bytes 393232 | tf_op jit(solution)/shard_map/psum | solution.py:28
  479.9 4.3 collective-permute-start
  484.2 1.9 collective-permute-start.1
  487.0 5.8 collective-permute-done.1
  492.8 2.7 collective-permute-start.2
  497.4 3.6 collective-permute-done.3
  504.1 1.8 copy.54
  505.9 2.3 multiply_convert_fusion.1
  509.2 1.9 collective-permute-start.4
  511.2 3.6 collective-permute-start.5
  515.8 1.6 collective-permute-done.5
  517.6 4.6 collective-permute-start.6
  522.2 1.9 collective-permute-start.7
  524.2 3.7 collective-permute-done.7
  527.9 3.5 collective-permute-start.8
  532.9 4.2 collective-permute-done.9
  540.1 2.1 convolution_bitcast_fusion.1
  543.3 3.3 collective-permute-start.10
  546.6 2.5 collective-permute-start.11
  549.2 3.1 collective-permute-done.11
  552.3 2.9 collective-permute-start.12
  555.2 1.8 collective-permute-start.13
  557.0 1.6 fusion.47
  558.6 2.3 collective-permute-done.13
  562.0 1.6 fusion.60
  563.6 4.7 convolution_bitcast_fusion
  568.2 8.1 %copy.58 = f32[64,32,2,64,2]{0,4,3,2,1:T(2,128)} copy(f32[64,32,2,64,2]{0,3,4,2,1:T(8,128)} %convolution_bitcast_fusion) | data formatting | bytes 4194304 | tf_op jit(solution)/shard_map/aboc,cxy->oxayb/transpose | solution.py:58
  576.3 3.8 copy.59
  580.1 1.9 add_convert_fusion
  582.0 1.5 fusion.242
  583.6 2.4 copy.60
  585.9 4.8 collective-permute-start.14
  592.0 2.1 collective-permute-start.15
  594.1 1.7 copy.62
  595.8 1.8 collective-permute-done.15
  597.6 2.6 copy.63
  601.1 2.3 collective-permute-start.16
  606.1 3.1 collective-permute-done.17
  609.2 2.8 pad_maximum_fusion.4
  617.1 2.4 copy.66
  619.5 4.4 collective-permute-start.18
  625.2 2.1 collective-permute-start.19
  627.6 1.7 copy.68
  630.8 2.6 copy.69
  634.3 1.9 collective-permute-start.20
  637.6 2.3 fusion.34
  639.9 2.2 collective-permute-done.21
  642.1 2.8 maximum_maximum_fusion.1
  (107 shorter events, 37.7 us)
Async XLA Ops:
  7.2 489.6 %copy-start = (f32[256,448]{0,1:T(8,128)S(1)}, f32[256,448]{0,1:T(8,128)}, u32[]{:S(2)}) copy-start(f32[256,448]{0,1:T(8,128)} %param.22) | copy-start | bytes 1376260
  7.2 471.5 %all-reduce.2.cloned.1.call-start = ((), (), s32[]{:S(2)}) async-start(), calls=%async_computation | async-start | bytes 786432 | tf_op jit(solution)/shard_map/psum | solution.py:28
  10.3 491.3 %copy-start.8 = (bf16[3,64,18]{1,2,0:T(8,128)(2,1)S(1)}, bf16[3,64,18]{1,2,0:T(8,128)(2,1)}, u32[]{:S(2)}) copy-start(bf16[3,64,18]{1,2,0:T(8,128)(2,1)} %param.23) | copy-start | bytes 20740
  479.9 7.1 %collective-permute-start = (bf16[6,64,1]{2,0,1:T(8,128)(2,1)S(1)}, bf16[6,64,1]{2,0,1:T(8,128)(2,1)S(1)}, u32[]{:S(2)}, u32[]{:S(2)}) collective-permute-start(bf16[6,64,1]{2,0,1:T(8,128)(2,1)S(1)} %get-tuple-element.68), channel_id=1, source_target_pairs={{0,4},{4,8},{8,12},{12,16},{16,20},{20,24},{24,28},{28,32},{32,36}... | collective-permute-start | bytes 2312 | tf_op jit(solution)/shard_map/ppermute | solution.py:18
  484.2 8.5 %collective-permute-start.1 = (bf16[6,64,1]{2,0,1:T(8,128)(2,1)S(1)}, bf16[6,64,1]{2,0,1:T(8,128)(2,1)S(1)}, u32[]{:S(2)}, u32[]{:S(2)}) collective-permute-start(bf16[6,64,1]{2,0,1:T(8,128)(2,1)S(1)} %get-tuple-element.69), channel_id=1, source_target_pairs={{4,0},{8,4},{12,8},{16,12},{20,16},{24,20},{28,24},{32,28},{36,32}... | collective-permute-start | bytes 2312 | tf_op jit(solution)/shard_map/ppermute | solution.py:21
  492.8 4.6 collective-permute-start.2
  495.5 5.5 collective-permute-start.3
  504.1 1.8 copy-start.13
  505.9 2.3 copy-start.11
  508.2 0.8 copy-start.7
  508.2 6.6 %copy-start.6 = (bf16[3,256,128]{2,1,0:T(8,128)(2,1)S(1)}, bf16[3,256,128]{2,1,0:T(8,128)(2,1)}, u32[]{:S(2)}) copy-start(bf16[3,256,128]{2,1,0:T(8,128)(2,1)} %param.27) | copy-start | bytes 589828
  509.2 6.3 collective-permute-start.4
  511.2 6.1 collective-permute-start.5
  517.6 6.6 %collective-permute-start.6 = (bf16[256,16,1]{0,2,1:T(2,128)(2,1)S(1)}, bf16[256,16,1]{0,2,1:T(2,128)(2,1)S(1)}, u32[]{:S(2)}, u32[]{:S(2)}) collective-permute-start(bf16[256,16,1]{0,2,1:T(2,128)(2,1)S(1)} %get-tuple-element.66), channel_id=1, source_target_pairs={{0,4},{4,8},{8,12},{12,16},{16,20},{20,24},{24,28},{28,32},{32,36}... | collective-permute-start | bytes 24584 | tf_op jit(solution)/shard_map/ppermute | solution.py:18
  522.2 5.6 collective-permute-start.7
  527.9 10.6 %copy-start.9 = (bf16[3,256,768]{2,1,0:T(8,128)(2,1)S(1)}, bf16[3,256,768]{2,1,0:T(8,128)(2,1)}, u32[]{:S(2)}) copy-start(bf16[3,256,768]{2,1,0:T(8,128)(2,1)} %param.28) | copy-start | bytes 3538948
  527.9 5.0 collective-permute-start.8
  531.5 5.7 collective-permute-start.9
  538.9 1.3 copy-start.4
  542.2 14.7 %copy-start.10 = (bf16[3,128,384]{2,1,0:T(8,128)(2,1)S(1)}, bf16[3,128,384]{2,1,0:T(8,128)(2,1)}, u32[]{:S(2)}) copy-start(bf16[3,128,384]{2,1,0:T(8,128)(2,1)} %param.30) | copy-start | bytes 884740
  543.3 5.9 collective-permute-start.10
  546.6 5.6 collective-permute-start.11
  552.3 6.3 collective-permute-start.12
  555.2 5.7 collective-permute-start.13
  561.9 1.6 copy-start.14
  585.9 8.1 %collective-permute-start.14 = (bf16[64,64,1]{1,0,2:T(8,128)(2,1)S(1)}, bf16[64,64,1]{1,0,2:T(8,128)(2,1)S(1)}, u32[]{:S(2)}, u32[]{:S(2)}) collective-permute-start(bf16[64,64,1]{1,0,2:T(8,128)(2,1)S(1)} %copy.60), channel_id=1, source_target_pairs={{0,4},{4,8},{8,12},{12,16},{16,20},{20,24},{24,28},{28,32},{32,36}... | collective-permute-start | bytes 24584 | tf_op jit(solution)/shard_map/ppermute | solution.py:18
  592.0 5.6 collective-permute-start.15
  595.8 8.9 %copy-start.12 = (bf16[3,64,192]{2,1,0:T(8,128)(2,1)S(1)}, bf16[3,64,192]{2,1,0:T(8,128)(2,1)}, u32[]{:S(2)}) copy-start(bf16[3,64,192]{2,1,0:T(8,128)(2,1)} %param.32) | copy-start | bytes 221188
  600.2 4.5 copy-start.2
  601.1 5.0 collective-permute-start.16
  603.4 5.8 collective-permute-start.17
  619.5 8.1 %collective-permute-start.18 = (bf16[64,64,1]{1,0,2:T(8,128)(2,1)S(1)}, bf16[64,64,1]{1,0,2:T(8,128)(2,1)S(1)}, u32[]{:S(2)}, u32[]{:S(2)}) collective-permute-start(bf16[64,64,1]{1,0,2:T(8,128)(2,1)S(1)} %copy.66), channel_id=1, source_target_pairs={{0,4},{4,8},{8,12},{12,16},{16,20},{20,24},{24,28},{28,32},{32,36}... | collective-permute-start | bytes 24584 | tf_op jit(solution)/shard_map/ppermute | solution.py:18
  625.2 5.6 collective-permute-start.19
  629.4 8.2 %copy-start.15 = (bf16[3,3,192]{2,1,0:T(4,128)(2,1)S(1)}, bf16[3,3,192]{2,1,0:T(4,128)(2,1)}, u32[]{:S(2)}) copy-start(bf16[3,3,192]{2,1,0:T(4,128)(2,1)} %param.33) | copy-start | bytes 10372
  633.4 4.2 copy-start.3
  634.3 5.5 collective-permute-start.20
  636.3 5.8 collective-permute-start.21
  647.1 0.8 copy-start.5
  647.1 2.2 copy-start.1
Sparse Core Ops, SparseCore 0:
  13.4 465.2 all-reduce.1
where the time goes:
time: 664 us; the launch traced here: 656 us
  waiting for transfers between devices  501 us (75%)
  starting transfers between devices  57.9 us (9%)
  local copies, waits for them, and re-layouts  43.2 us (7%)
  matrix products  25.5 us (4%)
  between operations  16.6 us (3%)
  other arithmetic  11.8 us (2%)
    psum x1, waiting for transfers between devices, spread_2(): return lax.psum(jnp.where(mine, array, jnp.zeros_like(array)), axis)  467 us
    ppermute x11, starting transfers between devices, with_halo(): lax.ppermute(lax.slice_in_dim(block, block.shape[dim] - width, None, axis...  36.7 us
    ppermute x11, waiting for transfers between devices, with_halo(): lax.ppermute(lax.slice_in_dim(block, 0, width, axis=dim), axis, backward)  32.6 us
    ppermute x11, starting transfers between devices, with_halo(): lax.ppermute(lax.slice_in_dim(block, 0, width, axis=dim), axis, backward)  21.1 us
    dot_general x13, matrix products, stencil(): jnp.einsum('ok,khs->ohs', weight[lift], stacked, preferred_element_type=j...  13.7 us
  transfers between devices with their start and end apart: 23, of which 15 were waited for; matrix products, arithmetic and copies ran while one was open for 2% of the time, Pallas kernels for 0%

commit v1 on v0

v1 whole, which is shorter than its diff:
```python
import math

import jax
import jax.numpy as jnp
from jax import lax
from jax.experimental import pallas as pl
from jax.experimental.pallas import tpu as pltpu
from jax.sharding import PartitionSpec as P

TSTEPS = 1000
STRIDE = 20
F32 = jnp.float32
BF16 = jnp.bfloat16
MESH = pl.DeviceIdType.MESH
HIGHEST = lax.Precision.HIGHEST


def nt(a, b):
    return lax.dot_general(a, b, (((1,), (1,)), ((), ())), preferred_element_type=F32)


def nn(a, b):
    return lax.dot_general(a, b, (((1,), (0,)), ((), ())), preferred_element_type=F32)


def silu(v):
    return v * (0.5 * jnp.tanh(0.5 * v) + 0.5)


def iota(shape, dim):
    return lax.broadcasted_iota(jnp.int32, shape, dim)


def onehot(cond):
    return jnp.where(cond, 1.0, 0.0).astype(BF16)


def roll_rows(v, shift):
    return pltpu.roll(v.astype(F32), shift, v.ndim - 2).astype(BF16)


def plan_of(step):
    phase = (step / TSTEPS + 0.008) / 1.008 * (math.pi / 2.0)
    return jnp.cos(phase) ** 2


WINDOW = ((0, 128), (256, 512), (384, 640), (768, 896))


def phase_window(main, side, x):
    def flat(v):
        return v.reshape(288, v.shape[-1])

    return jnp.concatenate(
        [
            flat(main[x, :, :, :, 128:256]),
            flat(side[x, 1:10, :, :, 128:256]),
            flat(main[x + 1]),
            flat(side[x + 1, 1:10]),
            flat(main[x + 2, :, :, :, 0:128]),
            flat(side[x + 2, 1:10, :, :, 0:128]),
        ],
        axis=1,
    )


def put_phases(main, side, rows, b, v):
    main[rows, :, b] = v
    below, above = (slice(1, 10), slice(2, 11)) if b else (slice(0, 9), slice(1, 10))
    for low in (0, 128):
        side[rows, below, 1 - b, :, low : low + 64] = v[..., low : low + 64]
        side[rows, above, 1 - b, :, low + 64 : low + 128] = v[..., low + 64 : low + 128]


def close_phases(main, side):
    right = roll_rows(main[1:11, 8, 1], 1)
    left = roll_rows(main[1:11, 0, 0], 15)
    for low in (0, 128):
        side[1:11, 1, 0, :, low + 64 : low + 128] = right[..., low + 64 : low + 128]
        side[1:11, 9, 1, :, low : low + 64] = left[..., low : low + 64]
    main[0, :, :, :, 128:256] = roll_rows(main[10, :, :, :, 128:256], 4)
    side[0, 1:10, :, :, 128:256] = roll_rows(side[10, 1:10, :, :, 128:256], 4)
    main[11, :, :, :, 0:128] = roll_rows(main[1, :, :, :, 0:128], 12)
    side[11, 1:10, :, :, 0:128] = roll_rows(side[1, 1:10, :, :, 0:128], 12)


def body(
    sizes,
    noisy,
    slot,
    timestep,
    owner,
    w_embed,
    w_biases,
    w_enter,
    pool_fine,
    pool_mid,
    w_squeeze,
    w_across,
    w_middle,
    rise_mid,
    decode_mid,
    rise_fine,
    decode_fine,
    w_leave,
    noise_out,
    next_out,
    send_p,
    got_p,
    planef,
    heightf,
    send_h,
    got_h,
    rowsf,
    send_s,
    got_s,
    around,
    aroundf,
    entryf,
    tapf,
    tap,
    condf,
    bias,
    w_in,
    w_pf,
    w_pm,
    w_ac,
    w_dm,
    w_df,
    leavef,
    w_lv,
    mask,
    h1,
    d1,
    d2,
    sq,
    mx,
    c3,
    v2,
    f1m,
    f1s,
    f2m,
    f2s,
    acc,
    turned,
    outf,
    guess,
    sem_p,
    sem_h,
    sem_s,
    sem_n,
    sem_x,
):
    planes, spans, heights = sizes
    p, s, h = (lax.axis_index(a) for a in ("plane", "span", "height"))

    def at(dp, ds, dh):
        return (
            lax.rem(p + (dp + planes), planes),
            lax.rem(s + (ds + spans), spans),
            lax.rem(h + (dh + heights), heights),
        )

    barrier = pltpu.get_barrier_semaphore()
    partners = [(k, 0, 0) for k in range(1, planes)]
    partners += [(0, k, 0) for k in range(1, spans)]
    partners += [(0, 0, k) for k in range(1, heights)]
    partners += [(0, ds, dh) for ds in (-1, 1) for dh in (-1, 1)]
    for offset in partners:
        pl.semaphore_signal(barrier, inc=1, device_id=at(*offset), device_id_type=MESH)
    pl.semaphore_wait(barrier, len(partners))

    def remote(src, dst, sems, index, offset):
        return pltpu.make_async_remote_copy(
            src_ref=src,
            dst_ref=dst,
            send_sem=sems.at[(0,) + index],
            recv_sem=sems.at[(1,) + index],
            device_id=at(*offset),
            device_id_type=MESH,
        )

    mine = (owner[0] == (p * spans + s) * heights + h).astype(F32)
    for k in range(planes):
        send_p[k] = (slot[0, k].astype(F32) * mine).astype(BF16)

    def copy_p(k):
        return remote(send_p.at[lax.rem(p + k, planes)], got_p.at[p], sem_p, (k,), (k, 0, 0))

    for k in range(1, planes):
        copy_p(k).start()
    got_p[p] = send_p[p]

    halo = []
    for ds in (-1, 0, 1):
        for dh in (-1, 0, 1):
            if ds == 0 and dh == 0:
                continue
            src = {-1: slice(0, 16), 0: slice(0, 64), 1: slice(48, 64)}[dh]
            dst = {-1: slice(80, 96), 0: slice(16, 80), 1: slice(0, 16)}[dh]
            halo.append(
                remote(
                    noisy.at[0, :, src], around.at[1 - ds, :, dst], sem_n, (len(halo),), (0, ds, dh)
                )
            )
    for copy in halo:
        copy.start()

    now_step = jnp.full((8, 128), timestep[0].astype(F32), F32)
    lane = iota((8, 64), 1)
    order = jnp.where(lane < 32, lane, lane - 32).astype(F32)
    angle = timestep[0].astype(F32) * jnp.exp(order * (-math.log(10000.0) / 32))
    waves = jnp.where(lane < 32, jnp.sin(angle), jnp.cos(angle))
    hidden = jnp.dot(waves, w_embed[...], precision=HIGHEST, preferred_element_type=F32)
    hidden = hidden / (1.0 + jnp.exp(-hidden))
    flat = jnp.dot(hidden, w_biases[...], precision=HIGHEST, preferred_element_type=F32)
    col = iota((448, 640), 1)
    pick = jnp.where(col < 256, lax.rem(col, 64), col - 192)
    pick = jnp.where(iota((448, 640), 0) == pick, 1.0, 0.0)
    bias[...] = jnp.dot(flat, pick, precision=HIGHEST, preferred_element_type=F32)

    w_df[...] = jnp.zeros_like(w_df)
    w_lv[...] = jnp.zeros_like(w_lv)
    leavef[...] = jnp.zeros_like(leavef)
    for b in (0, 1):
        place = iota((192, 256), 1)
        tapcol = lax.rem(place // 64 + 1, 4) - b
        spot = onehot(
            (tapcol >= 0)
            & (tapcol <= 2)
            & (iota((192, 256), 0) == tapcol * 64 + lax.rem(place, 64))
        )
        for lift in range(3):
            block = nn(decode_fine[lift], spot).astype(BF16)
            final = nn(w_leave[lift], spot)
            for a in (0, 1):
                first, second = WINDOW[a + lift]
                rows = slice(a * 128 + b * 64, a * 128 + b * 64 + 64)
                w_df[rows, first : first + 128] = block[:, 0:128]
                w_df[rows, second : second + 128] = block[:, 128:256]
                rows = slice(b * 8 + a * 3, b * 8 + a * 3 + 3)
                leavef[rows, first : first + 128] = final[:, 0:128]
                leavef[rows, second : second + 128] = final[:, 128:256]
    w_lv[144:160, :] = leavef[...].astype(BF16)

    total = None
    for k in range(4):
        spot = onehot(iota((64, 256), 1) == iota((64, 256), 0) + 64 * k)
        term = nn(pool_fine[k], spot)
        total = term if total is None else total + term
    w_pf[...] = total.astype(BF16)
    for k in range(4):
        w_pm[:, k * 128 : k * 128 + 128] = pool_mid[k]
    has_before = (p > 0).astype(F32)
    has_after = (p < planes - 1).astype(F32)
    w_ac[:, 0:128] = (w_across[0].astype(F32) * has_before).astype(BF16)
    w_ac[:, 128:256] = w_across[1]
    w_ac[:, 256:384] = (w_across[2].astype(F32) * has_after).astype(BF16)
    w_dm[...] = jnp.zeros_like(w_dm)
    for b in (0, 1):
        for lift in range(3):
            for step in range(3):
                spot = 512 * lift + 128 * ((b + step + 3) % 4)
                w_dm[b * 128 : b * 128 + 128, spot : spot + 128] = decode_mid[
                    lift, :, step * 128 : step * 128 + 128
                ]

    for a in (0, 1):
        for b in (0, 1):
            total = None
            for lift in range(3):
                k = iota((18, 1024), 0)
                tgt = (k // 6 + b) * 256 + (a + lift) * 8 + lax.rem(k, 6)
                term = nn(w_enter[lift], onehot(iota((18, 1024), 1) == tgt))
                total = term if total is None else total + term
            tapf[a * 128 + b * 64 : a * 128 + b * 64 + 64, :] = total

    def band(x, carry):
        for wc in range(4):
            lanes = slice(wc * 256, wc * 256 + 256)
            w_in[x, :, lanes] = pltpu.roll(tapf[0:256, lanes], 16 * x, 1).astype(BF16)
        return carry

    lax.fori_loop(0, 10, band, 0)

    shape = (5, 9, 16, 256)
    block = iota(shape, 2)
    row = (block // 4) * 5 + iota(shape, 0) - 2
    col = lax.rem(block, 4) * 9 + iota(shape, 1) - 2
    low_row, high_row = jnp.where(h == 0, 0, -9), jnp.where(h == heights - 1, 16, 99)
    low_col, high_col = jnp.where(s == 0, 0, -9), jnp.where(s == spans - 1, 32, 99)
    inside = (row >= low_row) & (row < high_row) & (col >= low_col) & (col < high_col)
    mask[...] = jnp.where(inside, 1.0, 0.0)

    for k in range(1, planes):
        copy_p(k).wait()
    planef[...] = jnp.zeros_like(planef)
    total = got_p[0].astype(F32)
    for k in range(1, planes):
        total = total + got_p[k].astype(F32)
    planef[:, 2:34, :] = total
    heightf[...] = jnp.zeros_like(heightf)
    for k in range(heights):
        for c in range(3):
            heightf[k, 12 * c : 12 * c + 12, :] = planef[c, 8 * k : 8 * k + 12, :]
    send_h[...] = heightf[...].astype(BF16)

    def copy_h(k):
        return remote(send_h.at[lax.rem(h + k, heights)], got_h.at[h], sem_h, (k,), (0, 0, k))

    for k in range(1, heights):
        copy_h(k).start()
    got_h[h] = send_h[h]

    for copy in halo:
        copy.wait()
    around[1, :, 16:80, :] = noisy[0]
    row = iota((96, 128), 0)
    rows_in = jnp.where((row >= jnp.where(h == 0, 16, 0)) & (row < jnp.where(h == heights - 1, 80, 96)), 1.0, 0.0)
    right = rows_in * (s < spans - 1).astype(F32)
    left = rows_in * (s > 0).astype(F32)
    near = iota((96, 128), 1) < 64
    entryf[...] = jnp.zeros_like(entryf)
    for c in range(3):
        aroundf[0] = around[1, c].astype(F32) * rows_in
        aroundf[1] = jnp.where(
            near, around[2, c].astype(F32) * right, around[0, c].astype(F32) * left
        )
        for rb in range(4):
            for part in range(2):
                entryf[2 * rb + part, pl.ds(c, 22, stride=8), :] = aroundf[
                    part, 7 + 20 * rb : 29 + 20 * rb, :
                ]
    entry = jnp.concatenate([entryf[k] for k in range(8)], axis=1).astype(BF16)
    line = iota((288, 1), 0)
    block = lax.rem(line, 16)
    cell = 36 * lax.rem(block, 4) + 2 * (line // 16) - 9
    for wc in range(4):
        tgt = (block // 4) * 256 + ((cell + wc) & 255)
        tapf[:, wc * 256 : wc * 256 + 256] = nt(onehot(iota((288, 1024), 1) == tgt), entry)

    for k in range(1, heights):
        copy_h(k).wait()
    total = got_h[0].astype(F32)
    for k in range(1, heights):
        total = total + got_h[k].astype(F32)
    rowsf[...] = total

    def window(k):
        dest = lax.rem(s + k, spans)
        lane = iota((8, 128), 1)
        total = jnp.zeros((8, 128), F32)
        for g in range(5):
            shift = lax.rem(24 * g + 2 - 16 * dest + 512, 256)
            moved = pltpu.roll(rowsf[8 * g : 8 * g + 8, :], shift, 1)[:, 0:128]
            total = jnp.where((lane >= 24 * g) & (lane < 24 * g + 20), moved, total)
        return total.astype(BF16)

    def copy_s(k):
        return remote(send_s.at[k], got_s.at[s], sem_s, (k,), (0, k, 0))

    def push(k, carry):
        send_s[k] = window(k)
        copy_s(k).start()
        return carry

    lax.fori_loop(1, spans, push, 0)
    got_s[s] = window(0)

    def take(k, carry):
        copy_s(k).wait()
        return carry

    lax.fori_loop(1, spans, take, 0)
    total = got_s[0].astype(F32)
    for k in range(1, spans):
        total = total + got_s[k].astype(F32)
    lane = iota((8, 128), 1)
    spot = lane - 24 * (lane // 24)
    outside = ((spot < 2) & (s == 0)) | ((spot >= 18) & (s == spans - 1))
    total = jnp.where(outside, 0.0, total)
    for g in range(5):
        part = total if g == 0 else pltpu.roll(total, 128 - 24 * g, 1)
        part = jnp.where(lane < 20, part, 0.0)
        for rb in range(4):
            condf[rb * 40 + 8 * g : rb * 40 + 8 * g + 8, :] = (
                part if rb == 0 else pltpu.roll(part, 32 * rb, 1)
            )
    line = iota((256, 160), 0)
    channel = lax.rem(line, 8) - 3
    m = iota((256, 160), 1)
    rb = m // 40
    tgt = channel * 12 + (rb * 20 + line // 8 + 7) // 8
    pick = (channel >= 0) & (channel < 3) & (line < 176) & (m - 40 * rb == tgt)
    lifted = nn(onehot(pick), condf[...].astype(BF16)).astype(BF16)
    line = iota((288, 1), 0)
    block = lax.rem(line, 16)
    cell = 36 * lax.rem(block, 4) + 2 * (line // 16) - 9
    for wc in range(4):
        tgt = (block // 4) * 32 + (cell + wc + 16) // 8
        lanes = slice(wc * 256, wc * 256 + 256)
        tap[:, lanes] = (
            tapf[:, lanes] + nt(onehot(iota((288, 128), 1) == tgt), lifted)
        ).astype(BF16)

    def copy_x(i, way):
        side = 0 if way == 1 else 2
        return remote(sq.at[1, i], sq.at[side, i], sem_x, (0 if way == 1 else 1, i), (way, 0, 0))

    def encode(i, carry):
        for a in (0, 1):
            x = 2 * i + a
            v = silu(nt(tap[...], w_in[x]) + bias[0:1, 0:256]).astype(BF16)
            h1[x] = v.reshape(9, 2, 16, 256)
            v = silu(nt(v, w_pf[...]) + bias[0:1, 256:384]).astype(BF16).reshape(9, 2, 16, 128)
            d1[x, :, :, 0:128] = v[:, 0]
            d1[x, :, :, 128:256] = v[:, 1]
        v = jnp.concatenate(
            [d1[2 * i].reshape(144, 256), d1[2 * i + 1].reshape(144, 256)], axis=1
        )
        v = silu(nt(v, w_pm[...]) + bias[0:1, 384:640]).astype(BF16)
        d2[i] = v.reshape(9, 16, 256)
        sq[1, i] = nt(v, w_squeeze[...]).astype(BF16).reshape(9, 16, 128)
        copy_x(i, 1).start()
        copy_x(i, -1).start()
        return carry

    lax.fori_loop(0, 5, encode, 0)

    def across(i, carry):
        copy_x(i, 1).wait()
        copy_x(i, -1).wait()
        v = jnp.concatenate([sq[t, i].reshape(144, 128) for t in range(3)], axis=1)
        v = nt(v, w_ac[...]).reshape(9, 16, 256) + d2[i].astype(F32)
        mx[i + 1, 1:10] = (v * mask[i]).astype(BF16)
        return carry

    lax.fori_loop(0, 5, across, 0)
    mx[1:6, 0] = roll_rows(mx[1:6, 9], 1)
    mx[1:6, 10] = roll_rows(mx[1:6, 1], 15)
    mx[0] = roll_rows(mx[5], 4)
    mx[6] = roll_rows(mx[1], 12)

    total = None
    for lift in range(3):
        v = jnp.concatenate(
            [mx[lift : lift + 5, step : step + 9].reshape(720, 256) for step in range(3)], axis=1
        )
        term = nt(v, w_middle[lift])
        total = term if total is None else total + term
    c3[...] = silu(total).astype(BF16).reshape(5, 9, 16, 256)

    def lift_mid(i, carry):
        v = nt(c3[i].reshape(144, 256), rise_mid[...].reshape(512, 256))
        for a in (0, 1):
            x = 2 * i + a
            u = v[:, a * 256 : a * 256 + 256].reshape(9, 16, 256) + d1[x].astype(F32)
            v2[x + 1, 1:10] = (u * mask[i]).astype(BF16)
        return carry

    lax.fori_loop(0, 5, lift_mid, 0)
    v2[1:11, 0, :, 128:256] = roll_rows(v2[1:11, 9, :, 128:256], 1)
    v2[1:11, 10, :, 0:128] = roll_rows(v2[1:11, 1, :, 0:128], 15)
    v2[0] = roll_rows(v2[10], 4)
    v2[11] = roll_rows(v2[1], 12)

    def decode_two(i, carry):
        parts = []
        for lift in range(3):
            rows = pl.ds(2 * i + lift, 2)
            parts.append(v2[rows, 1:10].reshape(288, 256))
            parts.append(v2[rows, 2:11, :, 0:128].reshape(288, 128))
            parts.append(v2[rows, 0:9, :, 128:256].reshape(288, 128))
        v = silu(nt(jnp.concatenate(parts, axis=1), w_dm[...])).astype(BF16)
        weight = rise_fine[...].reshape(256, 128)
        for b in (0, 1):
            u = nt(v[:, b * 128 : b * 128 + 128], weight).reshape(2, 9, 16, 256)
            u = u + h1[pl.ds(2 * i, 2), :, b].astype(F32)
            put_phases(f1m, f1s, pl.ds(2 * i + 1, 2), b, (u * mask[i]).astype(BF16))
        return carry

    lax.fori_loop(0, 5, decode_two, 0)
    close_phases(f1m, f1s)

    def decode_one(x, carry):
        v = silu(nt(phase_window(f1m, f1s, x), w_df[...])).reshape(9, 2, 16, 256)
        m = mask[x // 2]
        for b in (0, 1):
            put_phases(f2m, f2s, pl.ds(x + 1, 1), b, (v[:, b] * m).astype(BF16)[None])
        return carry

    lax.fori_loop(0, 10, decode_one, 0)
    close_phases(f2m, f2s)

    acc[...] = jnp.zeros_like(acc)

    def leave(x, carry):
        weight = w_lv[pl.ds(pl.multiple_of(144 - 16 * x, 16), 256), :]
        acc[...] += nt(phase_window(f2m, f2s, x), weight)
        return carry

    lax.fori_loop(0, 10, leave, 0)

    turned[...] = acc[...].T.reshape(16, 2, 8, 288)
    total = None
    for b in (0, 1):
        line = iota((288, 512), 0)
        lane = iota((288, 512), 1)
        block = lax.rem(line, 16)
        tgt = 36 * lax.rem(block, 4) + 2 * (line // 16) + b - 8
        spot = onehot((block // 4 == lane // 128) & (tgt == lax.rem(lane, 128)))
        term = nn(turned[0:10, b].reshape(80, 288).astype(BF16), spot)
        total = term if total is None else total + term
    for rb in range(4):
        outf[rb] = total[:, rb * 128 : rb * 128 + 128]
    for rb in range(4):
        begin, end = max(0, 4 - 10 * rb), min(10, 36 - 10 * rb)
        for a in (0, 1):
            for o in range(3):
                guess[o, pl.ds(20 * rb + 2 * begin + a - 8, end - begin, stride=2), :] = outf[
                    rb, pl.ds(8 * begin + 3 * a + o, end - begin, stride=8), :
                ]
    noise_out[0] = guess[...].astype(BF16)
    now = plan_of(now_step)[0:1, :]
    prior = plan_of(now_step - STRIDE)[0:1, :]
    for c in range(3):
        sample = noisy[0, c].astype(F32)
        clean = (sample - jnp.sqrt(1.0 - now) * guess[c]) / jnp.sqrt(now)
        next_out[0, c] = jnp.sqrt(prior) * clean + jnp.sqrt(1.0 - prior) * guess[c]


def solution(mesh):
    sizes = tuple(mesh.shape[a] for a in ("plane", "span", "height"))
    planes, spans, heights = sizes

    def shards(*args):
        in_vmem = pl.BlockSpec(memory_space=pltpu.VMEM)
        in_smem = pl.BlockSpec(memory_space=pltpu.SMEM)
        vmem = pltpu.VMEM
        scratch = [
            vmem((planes, 3, 32, 256), BF16),
            vmem((planes, 3, 32, 256), BF16),
            vmem((3, 40, 256), F32),
            vmem((heights, 48, 256), F32),
            vmem((heights, 48, 256), BF16),
            vmem((heights, 48, 256), BF16),
            vmem((48, 256), F32),
            vmem((spans, 8, 128), BF16),
            vmem((spans, 8, 128), BF16),
            vmem((3, 3, 96, 128), BF16),
            vmem((2, 96, 128), F32),
            vmem((8, 256, 128), F32),
            vmem((288, 1024), F32),
            vmem((288, 1024), BF16),
            vmem((160, 128), F32),
            vmem((8, 640), F32),
            vmem((10, 256, 1024), BF16),
            vmem((128, 256), BF16),
            vmem((256, 512), BF16),
            vmem((256, 384), BF16),
            vmem((256, 1536), BF16),
            vmem((256, 1024), BF16),
            vmem((16, 1024), F32),
            vmem((400, 1024), BF16),
            vmem((5, 9, 16, 256), F32),
            vmem((10, 9, 2, 16, 256), BF16),
            vmem((10, 9, 16, 256), BF16),
            vmem((5, 9, 16, 256), BF16),
            vmem((3, 5, 9, 16, 128), BF16),
            vmem((7, 11, 16, 256), BF16),
            vmem((5, 9, 16, 256), BF16),
            vmem((12, 11, 16, 256), BF16),
            vmem((12, 9, 2, 16, 256), BF16),
            vmem((12, 11, 2, 16, 256), BF16),
            vmem((12, 9, 2, 16, 256), BF16),
            vmem((12, 11, 2, 16, 256), BF16),
            vmem((288, 256), F32),
            vmem((16, 2, 8, 288), F32),
            vmem((4, 80, 128), F32),
            vmem((3, 64, 128), F32),
            pltpu.SemaphoreType.DMA((2, planes)),
            pltpu.SemaphoreType.DMA((2, heights)),
            pltpu.SemaphoreType.DMA((2, spans)),
            pltpu.SemaphoreType.DMA((2, 8)),
            pltpu.SemaphoreType.DMA((2, 2, 5)),
        ]
        return pl.pallas_call(
            lambda *refs: body(sizes, *refs),
            out_shape=(
                jax.ShapeDtypeStruct((1, 3, 64, 128), BF16),
                jax.ShapeDtypeStruct((1, 3, 64, 128), F32),
            ),
            in_specs=[in_vmem, in_vmem, in_smem, in_smem] + [in_vmem] * 13,
            out_specs=(in_vmem, in_vmem),
            scratch_shapes=scratch,
            compiler_params=pltpu.CompilerParams(
                collective_id=0, has_side_effects=True, vmem_limit_bytes=56 * 1024 * 1024
            ),
            name="denoise",
        )(*args)

    in_specs = (
        P("plane", None, "height", "span"),
        P(("plane", "span", "height"), None, None, None, None),
    ) + (P(),) * 15
    out_specs = (P("plane", None, "height", "span"), P("plane", None, "height", "span"))
    return jax.shard_map(shards, mesh=mesh, in_specs=in_specs, out_specs=out_specs, check_vma=False)
```

time: 664 us -> 71.9 us (0.11)
  the two profiles are of different devices: /device:TPU:66 before, /device:TPU:1 now
where the time goes in v1:
time: 71.9 us; the launch traced here: 71.5 us
  Pallas kernels  61.6 us (86%)
  local copies, waits for them, and re-layouts  8.01 us (11%)
  between operations  1.93 us (3%)
    pallas_call x1, Pallas kernels, shards(): pl.pallas_call(lambda *refs: body(sizes, *refs), out_shape=(jax.ShapeDtyp...  61.6 us
    unnamed x5, local copies, waits for them, and re-layouts  8.01 us

profile of v1, /device:TPU:1, one launch (start us, length us, event | category | flops | bytes accessed | tf_op | source)
XLA Modules:
  0.0 71.5 jit_solution(7994149115969898220)
XLA Ops:
  1.9 1.4 %copy.20.refs_6_ = bf16[3,64,18]{2,1,0:T(8,128)(2,1)} copy(bf16[3,64,18]{1,2,0:T(8,128)(2,1)} %param.23) | data formatting | bytes 13824 | tf_op args[6]
  3.4 1.6 %copy.21.refs_7_ = bf16[4,128,64]{2,1,0:T(8,128)(2,1)} copy(bf16[4,128,64]{1,2,0:T(8,128)(2,1)} %param.24) | data formatting | bytes 131072 | tf_op args[7]
  5.0 2.0 %copy.19.refs_5_ = f32[256,448]{1,0:T(8,128)} copy(f32[256,448]{0,1:T(8,128)} %param.22) | data formatting | bytes 917504 | tf_op args[5]
  7.0 61.6 %denoise.1 = (bf16[1,3,64,128]{3,2,1,0:T(8,128)(2,1)}, f32[1,3,64,128]{3,2,1,0:T(8,128)}) custom-call(bf16[1,3,64,128]{3,2,1,0:T(8,128)(2,1)} %refs_0_.1, bf16[1,8,3,32,256]{4,3,2,1,0:T(8,128)(2,1)} %refs_1_.1, s32[1]{0:T(128)S(6)} %copy.24.refs_2_, s32[1]{0:T(128)S(6)} %copy.25.refs_3_, f32[64,256]{1,0:T(8,128)} %refs_4_.1, f32[256,448]{1,0:T(8,128)} %copy.19.refs_5_, ...), custom_call_target="tpu_custom_call" | custom-call | tf_op jit(solution)/shard_map/denoise/pallas_call | solution.py:587
  68.6 1.4 %copy.26 = bf16[1,3,64,128]{3,2,1,0:T(8,128)(2,1)} copy(bf16[1,3,64,128]{3,2,1,0:T(8,128)(2,1)} %get-tuple-element.4) | data formatting | bytes 98304
  70.0 1.5 %copy.27 = f32[1,3,64,128]{3,2,1,0:T(8,128)} copy(f32[1,3,64,128]{3,2,1,0:T(8,128)} %get-tuple-element.5) | data formatting | bytes 196608

commit v2 on v1

--- a/solution.py
+++ b/solution.py
@@ -23,6 +23,10 @@
     return lax.dot_general(a, b, (((1,), (0,)), ((), ())), preferred_element_type=F32)
 
 
+def tn(a, b):
+    return lax.dot_general(a, b, (((0,), (0,)), ((), ())), preferred_element_type=F32)
+
+
 def silu(v):
     return v * (0.5 * jnp.tanh(0.5 * v) + 0.5)
 
@@ -47,18 +51,19 @@
 WINDOW = ((0, 128), (256, 512), (384, 640), (768, 896))
 
 
-def phase_window(main, side, x):
+def phase_window(main, side, x, n):
     def flat(v):
-        return v.reshape(288, v.shape[-1])
-
+        return v.reshape(n * 288, v.shape[-1])
+
+    above, here, below = slice(x, x + n), slice(x + 1, x + 1 + n), slice(x + 2, x + 2 + n)
     return jnp.concatenate(
         [
-            flat(main[x, :, :, :, 128:256]),
-            flat(side[x, 1:10, :, :, 128:256]),
-            flat(main[x + 1]),
-            flat(side[x + 1, 1:10]),
-            flat(main[x + 2, :, :, :, 0:128]),
-            flat(side[x + 2, 1:10, :, :, 0:128]),
+            flat(main[above, :, :, :, 128:256]),
+            flat(side[above, 1:10, :, :, 128:256]),
+            flat(main[here]),
+            flat(side[here, 1:10]),
+            flat(main[below, :, :, :, 0:128]),
+            flat(side[below, 1:10, :, :, 0:128]),
         ],
         axis=1,
     )
@@ -84,73 +89,17 @@
     side[11, 1:10, :, :, 0:128] = roll_rows(side[1, 1:10, :, :, 0:128], 12)
 
 
-def body(
-    sizes,
-    noisy,
-    slot,
-    timestep,
-    owner,
-    w_embed,
-    w_biases,
-    w_enter,
-    pool_fine,
-    pool_mid,
-    w_squeeze,
-    w_across,
-    w_middle,
-    rise_mid,
-    decode_mid,
-    rise_fine,
-    decode_fine,
-    w_leave,
-    noise_out,
-    next_out,
-    send_p,
-    got_p,
-    planef,
-    heightf,
-    send_h,
-    got_h,
-    rowsf,
-    send_s,
-    got_s,
-    around,
-    aroundf,
-    entryf,
-    tapf,
-    tap,
-    condf,
-    bias,
-    w_in,
-    w_pf,
-    w_pm,
-    w_ac,
-    w_dm,
-    w_df,
-    leavef,
-    w_lv,
-    mask,
-    h1,
-    d1,
-    d2,
-    sq,
-    mx,
-    c3,
-    v2,
-    f1m,
-    f1s,
-    f2m,
-    f2s,
-    acc,
-    turned,
-    outf,
-    guess,
-    sem_p,
-    sem_h,
-    sem_s,
-    sem_n,
-    sem_x,
-):
+def body(sizes, noisy_hbm, slot_hbm, timestep, owner, *refs):
+    weights_hbm, outputs, local, refs = refs[:13], refs[13:16], refs[16:31], refs[31:]
+    guess, kept, again = outputs
+    slot, noisy, *weights = local
+    (w_embed, w_biases, w_enter, pool_fine, pool_mid, w_squeeze, w_across) = weights[:7]
+    (w_middle, rise_mid, decode_mid, rise_fine, decode_fine, w_leave) = weights[7:]
+    (send_p, got_c, hold, got_p, planef, heightf, send_h, got_h, rowsf, send_s, got_s) = refs[:11]
+    (around, aroundf, entryf, tapf, tap, condf, bias, coef, bandf, w_in, w_pf, w_pm) = refs[11:23]
+    (w_ac, w_dm, w_df, leavef, w_lv, mask, mask2, h1, d1, d2, sq, mx, c3, v2) = refs[23:37]
+    (f1m, f1s, f2m, f2s, turned, outf) = refs[37:43]
+    (sem_w, sem_c, sem_p, sem_h, sem_s, sem_n, sem_x) = refs[43:]
     planes, spans, heights = sizes
     p, s, h = (lax.axis_index(a) for a in ("plane", "span", "height"))
 
@@ -161,15 +110,26 @@
             lax.rem(h + (dh + heights), heights),
         )
 
+    core = lax.rem(p, 2)
+    mate = 1 - 2 * core
+    chip = p // 2
+    chips = planes // 2
+
+    loads = [
+        pltpu.make_async_copy(src, dst, sem_w.at[k])
+        for k, (src, dst) in enumerate(zip((slot_hbm, noisy_hbm) + weights_hbm, local))
+    ]
+    for load in loads:
+        load.start()
+
     barrier = pltpu.get_barrier_semaphore()
-    partners = [(k, 0, 0) for k in range(1, planes)]
+    partners = [(mate, 0, 0), (-mate, 0, 0)]
+    partners += [(2 * k, 0, 0) for k in range(1, chips)]
     partners += [(0, k, 0) for k in range(1, spans)]
     partners += [(0, 0, k) for k in range(1, heights)]
     partners += [(0, ds, dh) for ds in (-1, 1) for dh in (-1, 1)]
     for offset in partners:
         pl.semaphore_signal(barrier, inc=1, device_id=at(*offset), device_id_type=MESH)
-    pl.semaphore_wait(barrier, len(partners))
-
     def remote(src, dst, sems, index, offset):
         return pltpu.make_async_remote_copy(
             src_ref=src,
@@ -180,16 +140,14 @@
             device_id_type=MESH,
         )
 
+    loads[0].wait()
+    loads[1].wait()
     mine = (owner[0] == (p * spans + s) * heights + h).astype(F32)
     for k in range(planes):
-        send_p[k] = (slot[0, k].astype(F32) * mine).astype(BF16)
-
-    def copy_p(k):
-        return remote(send_p.at[lax.rem(p + k, planes)], got_p.at[p], sem_p, (k,), (k, 0, 0))
-
-    for k in range(1, planes):
-        copy_p(k).start()
-    got_p[p] = send_p[p]
+        send_p[k % 2, k // 2] = (slot[0, k].astype(F32) * mine).astype(BF16)
+    pl.semaphore_wait(barrier, len(partners))
+    to_mate = remote(send_p.at[1 - core], got_c, sem_c, (0,), (mate, 0, 0))
+    to_mate.start()
 
     halo = []
     for ds in (-1, 0, 1):
@@ -206,14 +164,36 @@
     for copy in halo:
         copy.start()
 
+    to_mate.wait()
+    for k in range(chips):
+        hold[k] = (send_p[core, k].astype(F32) + got_c[k].astype(F32)).astype(BF16)
+
+    def copy_p(k):
+        dest = lax.rem(chip + k, chips)
+        return remote(hold.at[dest], got_p.at[chip], sem_p, (k,), (2 * k, 0, 0))
+
+    for k in range(1, chips):
+        copy_p(k).start()
+    got_p[chip] = hold[chip]
+    for load in loads[2:]:
+        load.wait()
+
     now_step = jnp.full((8, 128), timestep[0].astype(F32), F32)
+    now = plan_of(now_step)
+    prior = plan_of(now_step - STRIDE)
+    coef[0] = jnp.sqrt(1.0 - now)
+    coef[1] = jnp.sqrt(now)
+    coef[2] = jnp.sqrt(prior)
+    again[...] = jnp.broadcast_to(jnp.sqrt(1.0 - prior)[0:1], (64, 128))
     lane = iota((8, 64), 1)
     order = jnp.where(lane < 32, lane, lane - 32).astype(F32)
     angle = timestep[0].astype(F32) * jnp.exp(order * (-math.log(10000.0) / 32))
     waves = jnp.where(lane < 32, jnp.sin(angle), jnp.cos(angle))
     hidden = jnp.dot(waves, w_embed[...], precision=HIGHEST, preferred_element_type=F32)
     hidden = hidden / (1.0 + jnp.exp(-hidden))
-    flat = jnp.dot(hidden, w_biases[...], precision=HIGHEST, preferred_element_type=F32)
+    flat = lax.dot_general(
+        hidden, w_biases[...], (((1,), (1,)), ((), ())), HIGHEST, preferred_element_type=F32
+    )
     col = iota((448, 640), 1)
     pick = jnp.where(col < 256, lax.rem(col, 64), col - 192)
     pick = jnp.where(iota((448, 640), 0) == pick, 1.0, 0.0)
@@ -241,15 +221,14 @@
                 rows = slice(b * 8 + a * 3, b * 8 + a * 3 + 3)
                 leavef[rows, first : first + 128] = final[:, 0:128]
                 leavef[rows, second : second + 128] = final[:, 128:256]
-    w_lv[144:160, :] = leavef[...].astype(BF16)
-
-    total = None
+    final = leavef[...].astype(BF16)
+    for x in range(10):
+        for k, begin in enumerate((0, 128, 256, 512, 384, 640, 768, 896)):
+            spot = 512 * x + 128 * k
+            w_lv[16 * x : 16 * x + 16, spot : spot + 128] = final[:, begin : begin + 128]
+
     for k in range(4):
-        spot = onehot(iota((64, 256), 1) == iota((64, 256), 0) + 64 * k)
-        term = nn(pool_fine[k], spot)
-        total = term if total is None else total + term
-    w_pf[...] = total.astype(BF16)
-    for k in range(4):
+        w_pf[k * 64 : k * 64 + 64, :] = pool_fine[k]
         w_pm[:, k * 128 : k * 128 + 128] = pool_mid[k]
     has_before = (p > 0).astype(F32)
     has_after = (p < planes - 1).astype(F32)
@@ -269,19 +248,16 @@
         for b in (0, 1):
             total = None
             for lift in range(3):
-                k = iota((18, 1024), 0)
-                tgt = (k // 6 + b) * 256 + (a + lift) * 8 + lax.rem(k, 6)
-                term = nn(w_enter[lift], onehot(iota((18, 1024), 1) == tgt))
+                k = iota((18, 512), 0)
+                tgt = (k // 6 + b) * 128 + (a + lift) * 8 + lax.rem(k, 6)
+                term = tn(w_enter[lift], onehot(iota((18, 512), 1) == tgt))
                 total = term if total is None else total + term
-            tapf[a * 128 + b * 64 : a * 128 + b * 64 + 64, :] = total
-
-    def band(x, carry):
+            bandf[a * 128 + b * 64 : a * 128 + b * 64 + 64, :] = total
+    for x in range(7):
         for wc in range(4):
-            lanes = slice(wc * 256, wc * 256 + 256)
-            w_in[x, :, lanes] = pltpu.roll(tapf[0:256, lanes], 16 * x, 1).astype(BF16)
-        return carry
-
-    lax.fori_loop(0, 10, band, 0)
+            lanes = slice(wc * 128, wc * 128 + 128)
+            v = bandf[:, lanes]
+            w_in[x, :, lanes] = (v if x == 0 else pltpu.roll(v, 16 * x, 1)).astype(BF16)
 
     shape = (5, 9, 16, 256)
     block = iota(shape, 2)
@@ -291,12 +267,14 @@
     low_col, high_col = jnp.where(s == 0, 0, -9), jnp.where(s == spans - 1, 32, 99)
     inside = (row >= low_row) & (row < high_row) & (col >= low_col) & (col < high_col)
     mask[...] = jnp.where(inside, 1.0, 0.0)
-
-    for k in range(1, planes):
+    for x in range(10):
+        mask2[x] = mask[x // 2]
+
+    for k in range(1, chips):
         copy_p(k).wait()
     planef[...] = jnp.zeros_like(planef)
     total = got_p[0].astype(F32)
-    for k in range(1, planes):
+    for k in range(1, chips):
         total = total + got_p[k].astype(F32)
     planef[:, 2:34, :] = total
     heightf[...] = jnp.zeros_like(heightf)
@@ -337,7 +315,9 @@
     cell = 36 * lax.rem(block, 4) + 2 * (line // 16) - 9
     for wc in range(4):
         tgt = (block // 4) * 256 + ((cell + wc) & 255)
-        tapf[:, wc * 256 : wc * 256 + 256] = nt(onehot(iota((288, 1024), 1) == tgt), entry)
+        spot = onehot(iota((288, 1024), 1) == tgt)
+        for g in range(2):
+            tapf[g, :, wc * 128 : wc * 128 + 128] = nt(spot, entry[48 * g : 48 * g + 128])
 
     for k in range(1, heights):
         copy_h(k).wait()
@@ -346,32 +326,25 @@
         total = total + got_h[k].astype(F32)
     rowsf[...] = total
 
-    def window(k):
-        dest = lax.rem(s + k, spans)
-        lane = iota((8, 128), 1)
+    lane = iota((8, 128), 1)
+    for dest in range(spans):
         total = jnp.zeros((8, 128), F32)
         for g in range(5):
-            shift = lax.rem(24 * g + 2 - 16 * dest + 512, 256)
-            moved = pltpu.roll(rowsf[8 * g : 8 * g + 8, :], shift, 1)[:, 0:128]
+            shift = (24 * g + 2 - 16 * dest) % 256
+            v = rowsf[8 * g : 8 * g + 8, :]
+            moved = (pltpu.roll(v, shift, 1) if shift else v)[:, 0:128]
             total = jnp.where((lane >= 24 * g) & (lane < 24 * g + 20), moved, total)
-        return total.astype(BF16)
+        send_s[dest] = total.astype(BF16)
 
     def copy_s(k):
-        return remote(send_s.at[k], got_s.at[s], sem_s, (k,), (0, k, 0))
-
-    def push(k, carry):
-        send_s[k] = window(k)
+        return remote(send_s.at[lax.rem(s + k, spans)], got_s.at[s], sem_s, (k,), (0, k, 0))
+
+    for k in range(1, spans):
         copy_s(k).start()
-        return carry
-
-    lax.fori_loop(1, spans, push, 0)
-    got_s[s] = window(0)
-
-    def take(k, carry):
+    got_s[s] = send_s[s]
+
+    for k in range(1, spans):
         copy_s(k).wait()
-        return carry
-
-    lax.fori_loop(1, spans, take, 0)
     total = got_s[0].astype(F32)
     for k in range(1, spans):
         total = total + got_s[k].astype(F32)
@@ -398,21 +371,23 @@
     cell = 36 * lax.rem(block, 4) + 2 * (line // 16) - 9
     for wc in range(4):
         tgt = (block // 4) * 32 + (cell + wc + 16) // 8
-        lanes = slice(wc * 256, wc * 256 + 256)
-        tap[:, lanes] = (
-            tapf[:, lanes] + nt(onehot(iota((288, 128), 1) == tgt), lifted)
-        ).astype(BF16)
+        spot = onehot(iota((288, 128), 1) == tgt)
+        lanes = slice(wc * 128, wc * 128 + 128)
+        for g in range(2):
+            v = tapf[g, :, lanes] + nt(spot, lifted[48 * g : 48 * g + 128])
+            tap[g, :, lanes] = v.astype(BF16)
 
     def copy_x(i, way):
         side = 0 if way == 1 else 2
         return remote(sq.at[1, i], sq.at[side, i], sem_x, (0 if way == 1 else 1, i), (way, 0, 0))
 
-    def encode(i, carry):
+    for i in range(5):
         for a in (0, 1):
             x = 2 * i + a
-            v = silu(nt(tap[...], w_in[x]) + bias[0:1, 0:256]).astype(BF16)
+            v = nt(tap[x // 5], w_in[x - 3 * (x // 5)])
+            v = silu(v + bias[0:1, 0:256]).astype(BF16)
             h1[x] = v.reshape(9, 2, 16, 256)
-            v = silu(nt(v, w_pf[...]) + bias[0:1, 256:384]).astype(BF16).reshape(9, 2, 16, 128)
+            v = silu(nn(v, w_pf[...]) + bias[0:1, 256:384]).astype(BF16).reshape(9, 2, 16, 128)
             d1[x, :, :, 0:128] = v[:, 0]
             d1[x, :, :, 128:256] = v[:, 1]
         v = jnp.concatenate(
@@ -423,19 +398,13 @@
         sq[1, i] = nt(v, w_squeeze[...]).astype(BF16).reshape(9, 16, 128)
         copy_x(i, 1).start()
         copy_x(i, -1).start()
-        return carry
-
-    lax.fori_loop(0, 5, encode, 0)
-
-    def across(i, carry):
+
+    for i in range(5):
         copy_x(i, 1).wait()
         copy_x(i, -1).wait()
         v = jnp.concatenate([sq[t, i].reshape(144, 128) for t in range(3)], axis=1)
         v = nt(v, w_ac[...]).reshape(9, 16, 256) + d2[i].astype(F32)
         mx[i + 1, 1:10] = (v * mask[i]).astype(BF16)
-        return carry
-
-    lax.fori_loop(0, 5, across, 0)
     mx[1:6, 0] = roll_rows(mx[1:6, 9], 1)
     mx[1:6, 10] = roll_rows(mx[1:6, 1], 15)
     mx[0] = roll_rows(mx[5], 4)
@@ -450,58 +419,45 @@
         total = term if total is None else total + term
     c3[...] = silu(total).astype(BF16).reshape(5, 9, 16, 256)
 
-    def lift_mid(i, carry):
-        v = nt(c3[i].reshape(144, 256), rise_mid[...].reshape(512, 256))
-        for a in (0, 1):
-            x = 2 * i + a
-            u = v[:, a * 256 : a * 256 + 256].reshape(9, 16, 256) + d1[x].astype(F32)
-            v2[x + 1, 1:10] = (u * mask[i]).astype(BF16)
-        return carry
-
-    lax.fori_loop(0, 5, lift_mid, 0)
+    v = nt(c3[...].reshape(720, 256), rise_mid[...].reshape(512, 256)).reshape(5, 9, 16, 512)
+    for x in range(10):
+        u = v[x // 2, :, :, x % 2 * 256 : x % 2 * 256 + 256] + d1[x].astype(F32)
+        v2[x + 1, 1:10] = (u * mask2[x]).astype(BF16)
     v2[1:11, 0, :, 128:256] = roll_rows(v2[1:11, 9, :, 128:256], 1)
     v2[1:11, 10, :, 0:128] = roll_rows(v2[1:11, 1, :, 0:128], 15)
     v2[0] = roll_rows(v2[10], 4)
     v2[11] = roll_rows(v2[1], 12)
 
-    def decode_two(i, carry):
-        parts = []
-        for lift in range(3):
-            rows = pl.ds(2 * i + lift, 2)
-            parts.append(v2[rows, 1:10].reshape(288, 256))
-            parts.append(v2[rows, 2:11, :, 0:128].reshape(288, 128))
-            parts.append(v2[rows, 0:9, :, 128:256].reshape(288, 128))
-        v = silu(nt(jnp.concatenate(parts, axis=1), w_dm[...])).astype(BF16)
-        weight = rise_fine[...].reshape(256, 128)
+    parts = []
+    for lift in range(3):
+        rows = slice(lift, lift + 10)
+        parts.append(v2[rows, 1:10].reshape(1440, 256))
+        parts.append(v2[rows, 2:11, :, 0:128].reshape(1440, 128))
+        parts.append(v2[rows, 0:9, :, 128:256].reshape(1440, 128))
+    v = silu(nt(jnp.concatenate(parts, axis=1), w_dm[...])).astype(BF16)
+    weight = rise_fine[...].reshape(256, 128)
+    for b in (0, 1):
+        u = nt(v[:, b * 128 : b * 128 + 128], weight).reshape(10, 9, 16, 256)
+        u = u + h1[:, :, b].astype(F32)
+        put_phases(f1m, f1s, slice(1, 11), b, (u * mask2[...]).astype(BF16))
+    close_phases(f1m, f1s)
+
+    for x in range(0, 10, 5):
+        v = silu(nt(phase_window(f1m, f1s, x, 5), w_df[...])).reshape(5, 9, 2, 16, 256)
         for b in (0, 1):
-            u = nt(v[:, b * 128 : b * 128 + 128], weight).reshape(2, 9, 16, 256)
-            u = u + h1[pl.ds(2 * i, 2), :, b].astype(F32)
-            put_phases(f1m, f1s, pl.ds(2 * i + 1, 2), b, (u * mask[i]).astype(BF16))
-        return carry
-
-    lax.fori_loop(0, 5, decode_two, 0)
-    close_phases(f1m, f1s)
-
-    def decode_one(x, carry):
-        v = silu(nt(phase_window(f1m, f1s, x), w_df[...])).reshape(9, 2, 16, 256)
-        m = mask[x // 2]
-        for b in (0, 1):
-            put_phases(f2m, f2s, pl.ds(x + 1, 1), b, (v[:, b] * m).astype(BF16)[None])
-        return carry
-
-    lax.fori_loop(0, 10, decode_one, 0)
+            u = (v[:, :, b] * mask2[x : x + 5]).astype(BF16)
+            put_phases(f2m, f2s, slice(x + 1, x + 6), b, u)
     close_phases(f2m, f2s)
 
-    acc[...] = jnp.zeros_like(acc)
-
-    def leave(x, carry):
-        weight = w_lv[pl.ds(pl.multiple_of(144 - 16 * x, 16), 256), :]
-        acc[...] += nt(phase_window(f2m, f2s, x), weight)
-        return carry
-
-    lax.fori_loop(0, 10, leave, 0)
-
-    turned[...] = acc[...].T.reshape(16, 2, 8, 288)
+    parts = []
+    for x in range(12):
+        for low in (0, 128):
+            if (x, low) not in ((0, 0), (11, 128)):
+                parts.append(f2m[x, :, :, :, low : low + 128].reshape(288, 128))
+                parts.append(f2s[x, 1:10, :, :, low : low + 128].reshape(288, 128))
+    out = nt(jnp.concatenate(parts, axis=1), w_lv[...])
+
+    turned[...] = out.T.reshape(16, 2, 8, 288)
     total = None
     for b in (0, 1):
         line = iota((288, 512), 0)
@@ -520,13 +476,9 @@
                 guess[o, pl.ds(20 * rb + 2 * begin + a - 8, end - begin, stride=2), :] = outf[
                     rb, pl.ds(8 * begin + 3 * a + o, end - begin, stride=8), :
                 ]
-    noise_out[0] = guess[...].astype(BF16)
-    now = plan_of(now_step)[0:1, :]
-    prior = plan_of(now_step - STRIDE)[0:1, :]
     for c in range(3):
-        sample = noisy[0, c].astype(F32)
-        clean = (sample - jnp.sqrt(1.0 - now) * guess[c]) / jnp.sqrt(now)
-        next_out[0, c] = jnp.sqrt(prior) * clean + jnp.sqrt(1.0 - prior) * guess[c]
+        clean = (noisy[0, c].astype(F32) - coef[0, 0:1] * guess[c]) / coef[1, 0:1]
+        kept[c] = coef[2, 0:1] * clean
 
 
 def solution(mesh):
@@ -534,12 +486,20 @@
     planes, spans, heights = sizes
 
     def shards(*args):
+        args = list(args)
+        args[5] = args[5].T
+        args[6] = args[6].transpose(0, 2, 1)
+        args[7] = args[7].transpose(0, 2, 1)
         in_vmem = pl.BlockSpec(memory_space=pltpu.VMEM)
         in_smem = pl.BlockSpec(memory_space=pltpu.SMEM)
+        in_any = pl.BlockSpec(memory_space=pl.ANY)
         vmem = pltpu.VMEM
-        scratch = [
-            vmem((planes, 3, 32, 256), BF16),
-            vmem((planes, 3, 32, 256), BF16),
+        order = [1, 0] + list(range(4, 17))
+        scratch = [vmem(args[k].shape, args[k].dtype) for k in order] + [
+            vmem((2, planes // 2, 3, 32, 256), BF16),
+            vmem((planes // 2, 3, 32, 256), BF16),
+            vmem((planes // 2, 3, 32, 256), BF16),
+            vmem((planes // 2, 3, 32, 256), BF16),
             vmem((3, 40, 256), F32),
             vmem((heights, 48, 256), F32),
             vmem((heights, 48, 256), BF16),
@@ -550,19 +510,22 @@
             vmem((3, 3, 96, 128), BF16),
             vmem((2, 96, 128), F32),
             vmem((8, 256, 128), F32),
-            vmem((288, 1024), F32),
-            vmem((288, 1024), BF16),
+            vmem((2, 288, 512), F32),
+            vmem((2, 288, 512), BF16),
             vmem((160, 128), F32),
             vmem((8, 640), F32),
-            vmem((10, 256, 1024), BF16),
-            vmem((128, 256), BF16),
+            vmem((3, 8, 128), F32),
+            vmem((256, 512), F32),
+            vmem((7, 256, 512), BF16),
+            vmem((256, 128), BF16),
             vmem((256, 512), BF16),
             vmem((256, 384), BF16),
             vmem((256, 1536), BF16),
             vmem((256, 1024), BF16),
             vmem((16, 1024), F32),
-            vmem((400, 1024), BF16),
+            vmem((256, 5632), BF16),
             vmem((5, 9, 16, 256), F32),
+            vmem((10, 9, 16, 256), F32),
             vmem((10, 9, 2, 16, 256), BF16),
             vmem((10, 9, 16, 256), BF16),
             vmem((5, 9, 16, 256), BF16),
@@ -574,30 +537,32 @@
             vmem((12, 11, 2, 16, 256), BF16),
             vmem((12, 9, 2, 16, 256), BF16),
             vmem((12, 11, 2, 16, 256), BF16),
-            vmem((288, 256), F32),
             vmem((16, 2, 8, 288), F32),
             vmem((4, 80, 128), F32),
-            vmem((3, 64, 128), F32),
-            pltpu.SemaphoreType.DMA((2, planes)),
+            pltpu.SemaphoreType.DMA((15,)),
+            pltpu.SemaphoreType.DMA((2, 1)),
+            pltpu.SemaphoreType.DMA((2, planes // 2)),
             pltpu.SemaphoreType.DMA((2, heights)),
             pltpu.SemaphoreType.DMA((2, spans)),
             pltpu.SemaphoreType.DMA((2, 8)),
             pltpu.SemaphoreType.DMA((2, 2, 5)),
         ]
-        return pl.pallas_call(
+        guess, kept, again = pl.pallas_call(
             lambda *refs: body(sizes, *refs),
             out_shape=(
-                jax.ShapeDtypeStruct((1, 3, 64, 128), BF16),
-                jax.ShapeDtypeStruct((1, 3, 64, 128), F32),
+                jax.ShapeDtypeStruct((3, 64, 128), F32),
+                jax.ShapeDtypeStruct((3, 64, 128), F32),
+                jax.ShapeDtypeStruct((64, 128), F32),
             ),
-            in_specs=[in_vmem, in_vmem, in_smem, in_smem] + [in_vmem] * 13,
-            out_specs=(in_vmem, in_vmem),
+            in_specs=[in_any, in_any, in_smem, in_smem] + [in_any] * 13,
+            out_specs=(in_vmem, in_vmem, in_vmem),
             scratch_shapes=scratch,
             compiler_params=pltpu.CompilerParams(
                 collective_id=0, has_side_effects=True, vmem_limit_bytes=56 * 1024 * 1024
             ),
             name="denoise",
         )(*args)
+        return guess[None].astype(BF16), (kept + again * guess)[None]
 
     in_specs = (
         P("plane", None, "height", "span"),

time: 71.9 us -> 57 us (0.79)
  Pallas kernels: 61.6 us -> 53.2 us
  local copies, waits for them, and re-layouts: 8.01 us -> 0 us
  other arithmetic: 0 us -> 1.67 us
    pallas_call x1, Pallas kernels: 61.6 us -> 53.2 us  [shards(): pl.pallas_call(lambda *refs: body(sizes, *refs), out_shape=(jax.ShapeDtyp...]
    unnamed x5 -> x0, local copies, waits for them, and re-layouts: 8.01 us -> none
    broadcast_in_dim x0 -> x1, other arithmetic: none -> 1.67 us  [shards(): return (guess[None].astype(BF16), (kept + again * guess)[None])]
where the time goes in v2:
time: 57 us; the launch traced here: 56.8 us
  Pallas kernels  53.2 us (93%)
  between operations  1.94 us (3%)
  other arithmetic  1.67 us (3%)
    pallas_call x1, Pallas kernels, shards(): pl.pallas_call(lambda *refs: body(sizes, *refs), out_shape=(jax.ShapeDtyp...  53.2 us
    broadcast_in_dim x1, other arithmetic, shards(): return (guess[None].astype(BF16), (kept + again * guess)[None])  1.67 us

profile of v2, /device:TPU:1, one launch (start us, length us, event | category | flops | bytes accessed | tf_op | source)
XLA Modules:
  0.0 56.8 jit_solution(3471193844730481832)
XLA Ops:
  1.9 53.2 %denoise.1 = (f32[3,64,128]{2,1,0:T(8,128)}, f32[3,64,128]{2,1,0:T(8,128)}, f32[64,128]{1,0:T(8,128)}) custom-call(bf16[1,3,64,128]{3,2,1,0:T(8,128)(2,1)} %refs_0_.1, bf16[1,8,3,32,256]{4,3,2,1,0:T(8,128)(2,1)} %refs_1_.1, s32[1]{0:T(128)S(6)} %copy.19.refs_2_, s32[1]{0:T(128)S(6)} %copy.20.refs_3_, f32[64,256]{1,0:T(8,128)} %refs_4_.1, ...), custom_call_target="tpu_custom_call" | custom-call | tf_op jit(solution)/shard_map/denoise/pallas_call | solution.py:550
  55.2 1.7 %add_bitcast_fusion = (f32[1,3,64,128]{3,2,1,0:T(8,128)}, bf16[1,3,64,128]{3,2,1,0:T(8,128)(2,1)}) fusion(f32[3,64,128]{2,1,0:T(8,128)} %get-tuple-element.6, f32[3,64,128]{2,1,0:T(8,128)} %get-tuple-element.5, f32[64,128]{1,0:T(8,128)} %get-tuple-element.7), kind=kLoop, calls=%fused_computation | loop fusion | flops 73728 | bytes 376832 | tf_op jit(solution)/shard_map/broadcast_in_dim | solution.py:565

commit v3 on v2

--- a/solution.py
+++ b/solution.py
@@ -69,24 +69,30 @@
     )
 
 
-def put_phases(main, side, rows, b, v):
+def put_phases(main, side, x, b, v):
+    rows = slice(x + 1, x + 1 + v.shape[0])
+    below, above = (slice(1, 10), slice(2, 11)) if b else (slice(0, 9), slice(1, 10))
+    edge = pltpu.roll(v[:, 8], 1, 1) if b else pltpu.roll(v[:, 0], 15, 1)
+    v, edge = v.astype(BF16), edge.astype(BF16)
     main[rows, :, b] = v
-    below, above = (slice(1, 10), slice(2, 11)) if b else (slice(0, 9), slice(1, 10))
     for low in (0, 128):
         side[rows, below, 1 - b, :, low : low + 64] = v[..., low : low + 64]
         side[rows, above, 1 - b, :, low + 64 : low + 128] = v[..., low + 64 : low + 128]
-
-
-def close_phases(main, side):
-    right = roll_rows(main[1:11, 8, 1], 1)
-    left = roll_rows(main[1:11, 0, 0], 15)
     for low in (0, 128):
-        side[1:11, 1, 0, :, low + 64 : low + 128] = right[..., low + 64 : low + 128]
-        side[1:11, 9, 1, :, low : low + 64] = left[..., low : low + 64]
+        if b:
+            side[rows, 1, 0, :, low + 64 : low + 128] = edge[..., low + 64 : low + 128]
+        else:
+            side[rows, 9, 1, :, low : low + 64] = edge[..., low : low + 64]
+
+
+def close_below(main, side):
+    main[11, :, :, :, 0:128] = roll_rows(main[1, :, :, :, 0:128], 12)
+    side[11, 1:10, :, :, 0:128] = roll_rows(side[1, 1:10, :, :, 0:128], 12)
+
+
+def close_above(main, side):
     main[0, :, :, :, 128:256] = roll_rows(main[10, :, :, :, 128:256], 4)
     side[0, 1:10, :, :, 128:256] = roll_rows(side[10, 1:10, :, :, 128:256], 4)
-    main[11, :, :, :, 0:128] = roll_rows(main[1, :, :, :, 0:128], 12)
-    side[11, 1:10, :, :, 0:128] = roll_rows(side[1, 1:10, :, :, 0:128], 12)
 
 
 def body(sizes, noisy_hbm, slot_hbm, timestep, owner, *refs):
@@ -95,11 +101,12 @@
     slot, noisy, *weights = local
     (w_embed, w_biases, w_enter, pool_fine, pool_mid, w_squeeze, w_across) = weights[:7]
     (w_middle, rise_mid, decode_mid, rise_fine, decode_fine, w_leave) = weights[7:]
-    (send_p, got_c, hold, got_p, planef, heightf, send_h, got_h, rowsf, send_s, got_s) = refs[:11]
-    (around, aroundf, entryf, tapf, tap, condf, bias, coef, bandf, w_in, w_pf, w_pm) = refs[11:23]
-    (w_ac, w_dm, w_df, leavef, w_lv, mask, mask2, h1, d1, d2, sq, mx, c3, v2) = refs[23:37]
-    (f1m, f1s, f2m, f2s, turned, outf) = refs[37:43]
-    (sem_w, sem_c, sem_p, sem_h, sem_s, sem_n, sem_x) = refs[43:]
+    (send_p, got_c, planef, heightf, send_h, got_h, rowsf, send_s, got_s) = refs[:9]
+    refs = refs[9:]
+    (around, aroundf, entryf, tapf, tap, condf, bias, coef, bandf, w_in, w_pf, w_pm) = refs[:12]
+    (w_ac, w_dm, w_df, leavef, w_lv, mask, mask2, h1, d1, d2, sq, mx, c3, v2) = refs[12:26]
+    (f1m, f1s, f2m, f2s, turned, outf) = refs[26:32]
+    (sem_w, sem_c, sem_h, sem_s, sem_n, sem_x) = refs[32:]
     planes, spans, heights = sizes
     p, s, h = (lax.axis_index(a) for a in ("plane", "span", "height"))
 
@@ -124,9 +131,8 @@
 
     barrier = pltpu.get_barrier_semaphore()
     partners = [(mate, 0, 0), (-mate, 0, 0)]
-    partners += [(2 * k, 0, 0) for k in range(1, chips)]
+    partners += [(2 * j, 0, k) for j in range(chips) for k in range(heights) if j or k]
     partners += [(0, k, 0) for k in range(1, spans)]
-    partners += [(0, 0, k) for k in range(1, heights)]
     partners += [(0, ds, dh) for ds in (-1, 1) for dh in (-1, 1)]
     for offset in partners:
         pl.semaphore_signal(barrier, inc=1, device_id=at(*offset), device_id_type=MESH)
@@ -164,17 +170,26 @@
     for copy in halo:
         copy.start()
 
-    to_mate.wait()
-    for k in range(chips):
-        hold[k] = (send_p[core, k].astype(F32) + got_c[k].astype(F32)).astype(BF16)
-
-    def copy_p(k):
-        dest = lax.rem(chip + k, chips)
-        return remote(hold.at[dest], got_p.at[chip], sem_p, (k,), (2 * k, 0, 0))
-
-    for k in range(1, chips):
-        copy_p(k).start()
-    got_p[chip] = hold[chip]
+    heightf[...] = jnp.zeros_like(heightf)
+    to_mate.wait_recv()
+    planef[...] = jnp.zeros_like(planef)
+    for j in range(chips):
+        planef[j, :, 2:34, :] = send_p[core, j].astype(F32) + got_c[j].astype(F32)
+    for j in range(chips):
+        for k in range(heights):
+            for c in range(3):
+                heightf[12 * c : 12 * c + 12, :] = planef[j, c, 8 * k : 8 * k + 12, :]
+            send_h[j, k] = heightf[0:40, :].reshape(5, 8, 256).astype(BF16)
+
+    def copy_h(j, k):
+        src = send_h.at[lax.rem(chip + j, chips), lax.rem(h + k, heights)]
+        return remote(src, got_h.at[chip, h], sem_h, (j, k), (2 * j, 0, k))
+
+    rest = [(j, k) for j in (2, 1, 3, 0) for k in (2, 1, 3, 0) if (j, k) != (0, 0)]
+    rest = [(j, k) for j, k in rest if j < chips and k < heights]
+    for j, k in rest:
+        copy_h(j, k).start()
+    got_h[chip, h] = send_h[chip, h]
     for load in loads[2:]:
         load.wait()
 
@@ -270,28 +285,8 @@
     for x in range(10):
         mask2[x] = mask[x // 2]
 
-    for k in range(1, chips):
-        copy_p(k).wait()
-    planef[...] = jnp.zeros_like(planef)
-    total = got_p[0].astype(F32)
-    for k in range(1, chips):
-        total = total + got_p[k].astype(F32)
-    planef[:, 2:34, :] = total
-    heightf[...] = jnp.zeros_like(heightf)
-    for k in range(heights):
-        for c in range(3):
-            heightf[k, 12 * c : 12 * c + 12, :] = planef[c, 8 * k : 8 * k + 12, :]
-    send_h[...] = heightf[...].astype(BF16)
-
-    def copy_h(k):
-        return remote(send_h.at[lax.rem(h + k, heights)], got_h.at[h], sem_h, (k,), (0, 0, k))
-
-    for k in range(1, heights):
-        copy_h(k).start()
-    got_h[h] = send_h[h]
-
     for copy in halo:
-        copy.wait()
+        copy.wait_recv()
     around[1, :, 16:80, :] = noisy[0]
     row = iota((96, 128), 0)
     rows_in = jnp.where((row >= jnp.where(h == 0, 16, 0)) & (row < jnp.where(h == heights - 1, 80, 96)), 1.0, 0.0)
@@ -319,11 +314,13 @@
         for g in range(2):
             tapf[g, :, wc * 128 : wc * 128 + 128] = nt(spot, entry[48 * g : 48 * g + 128])
 
-    for k in range(1, heights):
-        copy_h(k).wait()
-    total = got_h[0].astype(F32)
-    for k in range(1, heights):
-        total = total + got_h[k].astype(F32)
+    for j, k in rest:
+        copy_h(j, k).wait_recv()
+    total = None
+    for j in range(chips):
+        for k in range(heights):
+            term = got_h[j, k].astype(F32)
+            total = term if total is None else total + term
     rowsf[...] = total
 
     lane = iota((8, 128), 1)
@@ -331,7 +328,7 @@
         total = jnp.zeros((8, 128), F32)
         for g in range(5):
             shift = (24 * g + 2 - 16 * dest) % 256
-            v = rowsf[8 * g : 8 * g + 8, :]
+            v = rowsf[g]
             moved = (pltpu.roll(v, shift, 1) if shift else v)[:, 0:128]
             total = jnp.where((lane >= 24 * g) & (lane < 24 * g + 20), moved, total)
         send_s[dest] = total.astype(BF16)
@@ -339,12 +336,13 @@
     def copy_s(k):
         return remote(send_s.at[lax.rem(s + k, spans)], got_s.at[s], sem_s, (k,), (0, k, 0))
 
-    for k in range(1, spans):
+    far = sorted(range(1, spans), key=lambda k: -min(k, spans - k))
+    for k in far:
         copy_s(k).start()
     got_s[s] = send_s[s]
 
-    for k in range(1, spans):
-        copy_s(k).wait()
+    for k in reversed(far):
+        copy_s(k).wait_recv()
     total = got_s[0].astype(F32)
     for k in range(1, spans):
         total = total + got_s[k].astype(F32)
@@ -381,7 +379,7 @@
         side = 0 if way == 1 else 2
         return remote(sq.at[1, i], sq.at[side, i], sem_x, (0 if way == 1 else 1, i), (way, 0, 0))
 
-    for i in range(5):
+    for i in (0, 4, 1, 2, 3):
         for a in (0, 1):
             x = 2 * i + a
             v = nt(tap[x // 5], w_in[x - 3 * (x // 5)])
@@ -399,16 +397,19 @@
         copy_x(i, 1).start()
         copy_x(i, -1).start()
 
-    for i in range(5):
-        copy_x(i, 1).wait()
-        copy_x(i, -1).wait()
+    for i in (0, 4, 1, 2, 3):
+        copy_x(i, 1).wait_recv()
+        copy_x(i, -1).wait_recv()
         v = jnp.concatenate([sq[t, i].reshape(144, 128) for t in range(3)], axis=1)
         v = nt(v, w_ac[...]).reshape(9, 16, 256) + d2[i].astype(F32)
-        mx[i + 1, 1:10] = (v * mask[i]).astype(BF16)
-    mx[1:6, 0] = roll_rows(mx[1:6, 9], 1)
-    mx[1:6, 10] = roll_rows(mx[1:6, 1], 15)
-    mx[0] = roll_rows(mx[5], 4)
-    mx[6] = roll_rows(mx[1], 12)
+        v = v * mask[i]
+        mx[i + 1, 1:10] = v.astype(BF16)
+        mx[i + 1, 0] = pltpu.roll(v[8], 1, 0).astype(BF16)
+        mx[i + 1, 10] = pltpu.roll(v[0], 15, 0).astype(BF16)
+        if i == 0:
+            mx[6] = roll_rows(mx[1], 12)
+        if i == 4:
+            mx[0] = roll_rows(mx[5], 4)
 
     total = None
     for lift in range(3):
@@ -420,34 +421,43 @@
     c3[...] = silu(total).astype(BF16).reshape(5, 9, 16, 256)
 
     v = nt(c3[...].reshape(720, 256), rise_mid[...].reshape(512, 256)).reshape(5, 9, 16, 512)
-    for x in range(10):
+    for x in (0, 9, 1, 2, 3, 4, 5, 6, 7, 8):
         u = v[x // 2, :, :, x % 2 * 256 : x % 2 * 256 + 256] + d1[x].astype(F32)
-        v2[x + 1, 1:10] = (u * mask2[x]).astype(BF16)
-    v2[1:11, 0, :, 128:256] = roll_rows(v2[1:11, 9, :, 128:256], 1)
-    v2[1:11, 10, :, 0:128] = roll_rows(v2[1:11, 1, :, 0:128], 15)
-    v2[0] = roll_rows(v2[10], 4)
-    v2[11] = roll_rows(v2[1], 12)
-
-    parts = []
-    for lift in range(3):
-        rows = slice(lift, lift + 10)
-        parts.append(v2[rows, 1:10].reshape(1440, 256))
-        parts.append(v2[rows, 2:11, :, 0:128].reshape(1440, 128))
-        parts.append(v2[rows, 0:9, :, 128:256].reshape(1440, 128))
-    v = silu(nt(jnp.concatenate(parts, axis=1), w_dm[...])).astype(BF16)
+        u = u * mask2[x]
+        v2[x + 1, 1:10] = u.astype(BF16)
+        v2[x + 1, 0, :, 128:256] = pltpu.roll(u[8, :, 128:256], 1, 0).astype(BF16)
+        v2[x + 1, 10, :, 0:128] = pltpu.roll(u[0, :, 0:128], 15, 0).astype(BF16)
+        if x == 0:
+            v2[11] = roll_rows(v2[1], 12)
+        if x == 9:
+            v2[0] = roll_rows(v2[10], 4)
+
     weight = rise_fine[...].reshape(256, 128)
-    for b in (0, 1):
-        u = nt(v[:, b * 128 : b * 128 + 128], weight).reshape(10, 9, 16, 256)
-        u = u + h1[:, :, b].astype(F32)
-        put_phases(f1m, f1s, slice(1, 11), b, (u * mask2[...]).astype(BF16))
-    close_phases(f1m, f1s)
-
-    for x in range(0, 10, 5):
-        v = silu(nt(phase_window(f1m, f1s, x, 5), w_df[...])).reshape(5, 9, 2, 16, 256)
+    for i in (0, 4, 1, 2, 3):
+        parts = []
+        for lift in range(3):
+            rows = slice(2 * i + lift, 2 * i + lift + 2)
+            parts.append(v2[rows, 1:10].reshape(288, 256))
+            parts.append(v2[rows, 2:11, :, 0:128].reshape(288, 128))
+            parts.append(v2[rows, 0:9, :, 128:256].reshape(288, 128))
+        v = silu(nt(jnp.concatenate(parts, axis=1), w_dm[...])).astype(BF16)
         for b in (0, 1):
-            u = (v[:, :, b] * mask2[x : x + 5]).astype(BF16)
-            put_phases(f2m, f2s, slice(x + 1, x + 6), b, u)
-    close_phases(f2m, f2s)
+            u = nt(v[:, b * 128 : b * 128 + 128], weight).reshape(2, 9, 16, 256)
+            u = u + h1[2 * i : 2 * i + 2, :, b].astype(F32)
+            put_phases(f1m, f1s, 2 * i, b, u * mask2[2 * i : 2 * i + 2])
+        if i == 0:
+            close_below(f1m, f1s)
+        if i == 4:
+            close_above(f1m, f1s)
+
+    for x in (0, 9, 1, 2, 3, 4, 5, 6, 7, 8):
+        v = silu(nt(phase_window(f1m, f1s, x, 1), w_df[...])).reshape(1, 9, 2, 16, 256)
+        for b in (0, 1):
+            put_phases(f2m, f2s, x, b, v[:, :, b] * mask2[x : x + 1])
+        if x == 0:
+            close_below(f2m, f2s)
+        if x == 9:
+            close_above(f2m, f2s)
 
     parts = []
     for x in range(12):
@@ -480,6 +490,17 @@
         clean = (noisy[0, c].astype(F32) - coef[0, 0:1] * guess[c]) / coef[1, 0:1]
         kept[c] = coef[2, 0:1] * clean
 
+    to_mate.wait_send()
+    for copy in halo:
+        copy.wait_send()
+    for j, k in rest:
+        copy_h(j, k).wait_send()
+    for k in far:
+        copy_s(k).wait_send()
+    for i in range(5):
+        copy_x(i, 1).wait_send()
+        copy_x(i, -1).wait_send()
+
 
 def solution(mesh):
     sizes = tuple(mesh.shape[a] for a in ("plane", "span", "height"))
@@ -498,13 +519,11 @@
         scratch = [vmem(args[k].shape, args[k].dtype) for k in order] + [
             vmem((2, planes // 2, 3, 32, 256), BF16),
             vmem((planes // 2, 3, 32, 256), BF16),
-            vmem((planes // 2, 3, 32, 256), BF16),
-            vmem((planes // 2, 3, 32, 256), BF16),
-            vmem((3, 40, 256), F32),
-            vmem((heights, 48, 256), F32),
-            vmem((heights, 48, 256), BF16),
-            vmem((heights, 48, 256), BF16),
+            vmem((planes // 2, 3, 40, 256), F32),
             vmem((48, 256), F32),
+            vmem((planes // 2, heights, 5, 8, 256), BF16),
+            vmem((planes // 2, heights, 5, 8, 256), BF16),
+            vmem((5, 8, 256), F32),
             vmem((spans, 8, 128), BF16),
             vmem((spans, 8, 128), BF16),
             vmem((3, 3, 96, 128), BF16),
@@ -541,8 +560,7 @@
             vmem((4, 80, 128), F32),
             pltpu.SemaphoreType.DMA((15,)),
             pltpu.SemaphoreType.DMA((2, 1)),
-            pltpu.SemaphoreType.DMA((2, planes // 2)),
-            pltpu.SemaphoreType.DMA((2, heights)),
+            pltpu.SemaphoreType.DMA((2, planes // 2, heights)),
             pltpu.SemaphoreType.DMA((2, spans)),
             pltpu.SemaphoreType.DMA((2, 8)),
             pltpu.SemaphoreType.DMA((2, 2, 5)),

time: 57 us -> 54.5 us (0.956)
  Pallas kernels: 53.2 us -> 50.7 us
    pallas_call x1, Pallas kernels: 53.2 us -> 50.7 us  [shards(): pl.pallas_call(lambda *refs: body(sizes, *refs), out_shape=(jax.ShapeDtyp...]
where the time goes in v3:
time: 54.5 us; the launch traced here: 54.3 us
  Pallas kernels  50.7 us (93%)
  between operations  1.93 us (4%)
  other arithmetic  1.67 us (3%)
    pallas_call x1, Pallas kernels, shards(): pl.pallas_call(lambda *refs: body(sizes, *refs), out_shape=(jax.ShapeDtyp...  50.7 us
    broadcast_in_dim x1, other arithmetic, shards(): return (guess[None].astype(BF16), (kept + again * guess)[None])  1.67 us

profile of v3, /device:TPU:1, one launch (start us, length us, event | category | flops | bytes accessed | tf_op | source)
XLA Modules:
  0.0 54.3 jit_solution(12700169554703962)
XLA Ops:
  1.9 50.7 %denoise.1 = (f32[3,64,128]{2,1,0:T(8,128)}, f32[3,64,128]{2,1,0:T(8,128)}, f32[64,128]{1,0:T(8,128)}) custom-call(bf16[1,3,64,128]{3,2,1,0:T(8,128)(2,1)} %refs_0_.1, bf16[1,8,3,32,256]{4,3,2,1,0:T(8,128)(2,1)} %refs_1_.1, s32[1]{0:T(128)S(6)} %copy.19.refs_2_, s32[1]{0:T(128)S(6)} %copy.20.refs_3_, f32[64,256]{1,0:T(8,128)} %refs_4_.1, ...), custom_call_target="tpu_custom_call" | custom-call | tf_op jit(solution)/shard_map/denoise/pallas_call | solution.py:568
  52.6 1.7 %add_bitcast_fusion = (f32[1,3,64,128]{3,2,1,0:T(8,128)}, bf16[1,3,64,128]{3,2,1,0:T(8,128)(2,1)}) fusion(f32[3,64,128]{2,1,0:T(8,128)} %get-tuple-element.6, f32[3,64,128]{2,1,0:T(8,128)} %get-tuple-element.5, f32[64,128]{1,0:T(8,128)} %get-tuple-element.7), kind=kLoop, calls=%fused_computation | loop fusion | flops 73728 | bytes 376832 | tf_op jit(solution)/shard_map/broadcast_in_dim | solution.py:583

commit v4 on v3

--- a/solution.py
+++ b/solution.py
@@ -101,12 +101,12 @@
     slot, noisy, *weights = local
     (w_embed, w_biases, w_enter, pool_fine, pool_mid, w_squeeze, w_across) = weights[:7]
     (w_middle, rise_mid, decode_mid, rise_fine, decode_fine, w_leave) = weights[7:]
-    (send_p, got_c, planef, heightf, send_h, got_h, rowsf, send_s, got_s) = refs[:9]
-    refs = refs[9:]
+    (send_p, got_c, planef, heightf, send_h, got_h, rowsf, send_s, got_s, send_t, got_t) = refs[:11]
+    refs = refs[11:]
     (around, aroundf, entryf, tapf, tap, condf, bias, coef, bandf, w_in, w_pf, w_pm) = refs[:12]
-    (w_ac, w_dm, w_df, leavef, w_lv, mask, mask2, h1, d1, d2, sq, mx, c3, v2) = refs[12:26]
-    (f1m, f1s, f2m, f2s, turned, outf) = refs[26:32]
-    (sem_w, sem_c, sem_h, sem_s, sem_n, sem_x) = refs[32:]
+    (w_ac, w_dm, w_df, leavef, w_lv, mask, mask2, h1, d1, d2, sq, mx, c3, v2, e2) = refs[12:27]
+    (f1m, f1s, f2m, f2s, turned, outf) = refs[27:33]
+    (sem_w, sem_c, sem_h, sem_s, sem_n, sem_x) = refs[33:]
     planes, spans, heights = sizes
     p, s, h = (lax.axis_index(a) for a in ("plane", "span", "height"))
 
@@ -132,8 +132,11 @@
     barrier = pltpu.get_barrier_semaphore()
     partners = [(mate, 0, 0), (-mate, 0, 0)]
     partners += [(2 * j, 0, k) for j in range(chips) for k in range(heights) if j or k]
-    partners += [(0, k, 0) for k in range(1, spans)]
-    partners += [(0, ds, dh) for ds in (-1, 1) for dh in (-1, 1)]
+    seat = [lax.rem(s, 4), s // 4]
+    inner = [lax.rem(seat[0] + k, 4) - seat[0] for k in range(1, 4)]
+    partners += [(0, ds, 0) for ds in inner]
+    partners += [(0, 4 * k, 0) for k in range(1, spans // 4)]
+    partners += [(0, 1, 0), (0, -1, 0)]
     for offset in partners:
         pl.semaphore_signal(barrier, inc=1, device_id=at(*offset), device_id_type=MESH)
     def remote(src, dst, sems, index, offset):
@@ -152,44 +155,51 @@
     for k in range(planes):
         send_p[k % 2, k // 2] = (slot[0, k].astype(F32) * mine).astype(BF16)
     pl.semaphore_wait(barrier, len(partners))
-    to_mate = remote(send_p.at[1 - core], got_c, sem_c, (0,), (mate, 0, 0))
-    to_mate.start()
-
-    halo = []
-    for ds in (-1, 0, 1):
-        for dh in (-1, 0, 1):
-            if ds == 0 and dh == 0:
-                continue
-            src = {-1: slice(0, 16), 0: slice(0, 64), 1: slice(48, 64)}[dh]
-            dst = {-1: slice(80, 96), 0: slice(16, 80), 1: slice(0, 16)}[dh]
-            halo.append(
-                remote(
-                    noisy.at[0, :, src], around.at[1 - ds, :, dst], sem_n, (len(halo),), (0, ds, dh)
-                )
-            )
-    for copy in halo:
-        copy.start()
+    pieces = [jj for jj in (2, 1, 3, 0) if jj < chips]
+
+    def copy_c(jj):
+        src = send_p.at[1 - core, lax.rem(chip + jj, chips)]
+        return remote(src, got_c.at[jj], sem_c, (jj,), (mate, 0, 0))
+
+    for jj in pieces:
+        copy_c(jj).start()
+
+    below = remote(
+        noisy.at[0, :, 48:64], around.at[1, :, 0:16], sem_n, (0,), (0, 0, 1)
+    )
+    above = remote(
+        noisy.at[0, :, 0:16], around.at[1, :, 80:96], sem_n, (1,), (0, 0, -1)
+    )
+    after = remote(around.at[1], around.at[0], sem_n, (2,), (0, 1, 0))
+    before = remote(around.at[1], around.at[2], sem_n, (3,), (0, -1, 0))
+    below.start()
+    above.start()
+    around[1, :, 16:80, :] = noisy[0]
 
     heightf[...] = jnp.zeros_like(heightf)
-    to_mate.wait_recv()
     planef[...] = jnp.zeros_like(planef)
-    for j in range(chips):
-        planef[j, :, 2:34, :] = send_p[core, j].astype(F32) + got_c[j].astype(F32)
-    for j in range(chips):
+
+    def copy_h(jj, k):
+        src = send_h.at[jj, lax.rem(h + k, heights)]
+        return remote(src, got_h.at[chip, h], sem_h, (jj, k), (2 * jj, 0, k))
+
+    rest = [(jj, k) for jj in pieces for k in (2, 1, 3, 0) if k < heights and (jj or k)]
+    for jj in pieces:
+        copy_c(jj).wait_recv()
+        sent = send_p[core, lax.rem(chip + jj, chips)].astype(F32)
+        planef[jj, :, 2:34, :] = sent + got_c[jj].astype(F32)
         for k in range(heights):
             for c in range(3):
-                heightf[12 * c : 12 * c + 12, :] = planef[j, c, 8 * k : 8 * k + 12, :]
-            send_h[j, k] = heightf[0:40, :].reshape(5, 8, 256).astype(BF16)
-
-    def copy_h(j, k):
-        src = send_h.at[lax.rem(chip + j, chips), lax.rem(h + k, heights)]
-        return remote(src, got_h.at[chip, h], sem_h, (j, k), (2 * j, 0, k))
-
-    rest = [(j, k) for j in (2, 1, 3, 0) for k in (2, 1, 3, 0) if (j, k) != (0, 0)]
-    rest = [(j, k) for j, k in rest if j < chips and k < heights]
-    for j, k in rest:
-        copy_h(j, k).start()
-    got_h[chip, h] = send_h[chip, h]
+                heightf[12 * c : 12 * c + 12, :] = planef[jj, c, 8 * k : 8 * k + 12, :]
+            send_h[jj, k] = heightf[0:40, :].reshape(5, 8, 256).astype(BF16)
+        for k in (2, 1, 3, 0):
+            if k < heights and (jj or k):
+                copy_h(jj, k).start()
+    got_h[chip, h] = send_h[0, h]
+    below.wait_recv()
+    above.wait_recv()
+    after.start()
+    before.start()
     for load in loads[2:]:
         load.wait()
 
@@ -285,9 +295,8 @@
     for x in range(10):
         mask2[x] = mask[x // 2]
 
-    for copy in halo:
-        copy.wait_recv()
-    around[1, :, 16:80, :] = noisy[0]
+    after.wait_recv()
+    before.wait_recv()
     row = iota((96, 128), 0)
     rows_in = jnp.where((row >= jnp.where(h == 0, 16, 0)) & (row < jnp.where(h == heights - 1, 80, 96)), 1.0, 0.0)
     right = rows_in * (s < spans - 1).astype(F32)
@@ -331,21 +340,35 @@
             v = rowsf[g]
             moved = (pltpu.roll(v, shift, 1) if shift else v)[:, 0:128]
             total = jnp.where((lane >= 24 * g) & (lane < 24 * g + 20), moved, total)
-        send_s[dest] = total.astype(BF16)
+        send_s[dest % 4, dest // 4] = total.astype(BF16)
+
+    spot_in, four = seat
 
     def copy_s(k):
-        return remote(send_s.at[lax.rem(s + k, spans)], got_s.at[s], sem_s, (k,), (0, k, 0))
-
-    far = sorted(range(1, spans), key=lambda k: -min(k, spans - k))
-    for k in far:
+        src = send_s.at[lax.rem(spot_in + k, 4)]
+        return remote(src, got_s.at[spot_in], sem_s, (0, k), (0, inner[k - 1], 0))
+
+    def copy_t(k):
+        src = send_t.at[lax.rem(four + k, spans // 4)]
+        return remote(src, got_t.at[four], sem_s, (1, k), (0, 4 * k, 0))
+
+    for k in range(1, 4):
         copy_s(k).start()
-    got_s[s] = send_s[s]
-
-    for k in reversed(far):
+    got_s[spot_in] = send_s[spot_in]
+    for k in range(1, 4):
         copy_s(k).wait_recv()
     total = got_s[0].astype(F32)
-    for k in range(1, spans):
+    for k in range(1, 4):
         total = total + got_s[k].astype(F32)
+    send_t[...] = total.astype(BF16)
+    for k in range(1, spans // 4):
+        copy_t(k).start()
+    got_t[four] = send_t[four]
+    for k in range(1, spans // 4):
+        copy_t(k).wait_recv()
+    total = got_t[0].astype(F32)
+    for k in range(1, spans // 4):
+        total = total + got_t[k].astype(F32)
     lane = iota((8, 128), 1)
     spot = lane - 24 * (lane // 24)
     outside = ((spot < 2) & (s == 0)) | ((spot >= 18) & (s == spans - 1))
@@ -375,31 +398,41 @@
             v = tapf[g, :, lanes] + nt(spot, lifted[48 * g : 48 * g + 128])
             tap[g, :, lanes] = v.astype(BF16)
 
-    def copy_x(i, way):
+    groups = ((0, 1, 2), (3, 4))
+
+    def copy_x(g, way):
+        rows = slice(groups[g][0], groups[g][-1] + 1)
         side = 0 if way == 1 else 2
-        return remote(sq.at[1, i], sq.at[side, i], sem_x, (0 if way == 1 else 1, i), (way, 0, 0))
-
-    for i in (0, 4, 1, 2, 3):
-        for a in (0, 1):
-            x = 2 * i + a
-            v = nt(tap[x // 5], w_in[x - 3 * (x // 5)])
-            v = silu(v + bias[0:1, 0:256]).astype(BF16)
-            h1[x] = v.reshape(9, 2, 16, 256)
-            v = silu(nn(v, w_pf[...]) + bias[0:1, 256:384]).astype(BF16).reshape(9, 2, 16, 128)
+        return remote(
+            sq.at[1, rows], sq.at[side, rows], sem_x, (0 if way == 1 else 1, g), (way, 0, 0)
+        )
+
+    for x in range(10):
+        v = nt(tap[x // 5], w_in[x - 3 * (x // 5)])
+        h1[x] = silu(v + bias[0:1, 0:256]).astype(BF16).reshape(9, 2, 16, 256)
+    for g, group in enumerate(groups):
+        for x in range(2 * group[0], 2 * group[-1] + 2):
+            v = nn(h1[x].reshape(288, 256), w_pf[...]) + bias[0:1, 256:384]
+            v = silu(v).astype(BF16).reshape(9, 2, 16, 128)
             d1[x, :, :, 0:128] = v[:, 0]
             d1[x, :, :, 128:256] = v[:, 1]
-        v = jnp.concatenate(
-            [d1[2 * i].reshape(144, 256), d1[2 * i + 1].reshape(144, 256)], axis=1
-        )
-        v = silu(nt(v, w_pm[...]) + bias[0:1, 384:640]).astype(BF16)
-        d2[i] = v.reshape(9, 16, 256)
-        sq[1, i] = nt(v, w_squeeze[...]).astype(BF16).reshape(9, 16, 128)
-        copy_x(i, 1).start()
-        copy_x(i, -1).start()
-
-    for i in (0, 4, 1, 2, 3):
-        copy_x(i, 1).wait_recv()
-        copy_x(i, -1).wait_recv()
+        n = 144 * len(group)
+        rows = slice(group[0], group[-1] + 1)
+        parts = [
+            jnp.concatenate([d1[2 * i + a].reshape(144, 256) for i in group], axis=0)
+            for a in (0, 1)
+        ]
+        v = silu(nt(jnp.concatenate(parts, axis=1), w_pm[...]) + bias[0:1, 384:640]).astype(BF16)
+        d2[rows] = v.reshape(len(group), 9, 16, 256)
+        v = nt(v, w_squeeze[...]).astype(BF16)
+        sq[1, rows] = v.reshape(len(group), 9, 16, 128)
+        copy_x(g, 1).start()
+        copy_x(g, -1).start()
+
+    for i in range(5):
+        if i in (0, 3):
+            copy_x(i // 3, 1).wait_recv()
+            copy_x(i // 3, -1).wait_recv()
         v = jnp.concatenate([sq[t, i].reshape(144, 128) for t in range(3)], axis=1)
         v = nt(v, w_ac[...]).reshape(9, 16, 256) + d2[i].astype(F32)
         v = v * mask[i]
@@ -441,8 +474,11 @@
             parts.append(v2[rows, 2:11, :, 0:128].reshape(288, 128))
             parts.append(v2[rows, 0:9, :, 128:256].reshape(288, 128))
         v = silu(nt(jnp.concatenate(parts, axis=1), w_dm[...])).astype(BF16)
+        e2[2 * i : 2 * i + 2] = v.reshape(2, 9, 16, 256)
+    for i in (0, 4, 1, 2, 3):
         for b in (0, 1):
-            u = nt(v[:, b * 128 : b * 128 + 128], weight).reshape(2, 9, 16, 256)
+            v = e2[2 * i : 2 * i + 2, :, :, b * 128 : b * 128 + 128].reshape(288, 128)
+            u = nt(v, weight).reshape(2, 9, 16, 256)
             u = u + h1[2 * i : 2 * i + 2, :, b].astype(F32)
             put_phases(f1m, f1s, 2 * i, b, u * mask2[2 * i : 2 * i + 2])
         if i == 0:
@@ -490,16 +526,19 @@
         clean = (noisy[0, c].astype(F32) - coef[0, 0:1] * guess[c]) / coef[1, 0:1]
         kept[c] = coef[2, 0:1] * clean
 
-    to_mate.wait_send()
-    for copy in halo:
+    for jj in pieces:
+        copy_c(jj).wait_send()
+    for copy in (below, above, after, before):
         copy.wait_send()
     for j, k in rest:
         copy_h(j, k).wait_send()
-    for k in far:
+    for k in range(1, 4):
         copy_s(k).wait_send()
-    for i in range(5):
-        copy_x(i, 1).wait_send()
-        copy_x(i, -1).wait_send()
+    for k in range(1, spans // 4):
+        copy_t(k).wait_send()
+    for g in range(2):
+        copy_x(g, 1).wait_send()
+        copy_x(g, -1).wait_send()
 
 
 def solution(mesh):
@@ -524,8 +563,10 @@
             vmem((planes // 2, heights, 5, 8, 256), BF16),
             vmem((planes // 2, heights, 5, 8, 256), BF16),
             vmem((5, 8, 256), F32),
-            vmem((spans, 8, 128), BF16),
-            vmem((spans, 8, 128), BF16),
+            vmem((4, spans // 4, 8, 128), BF16),
+            vmem((4, spans // 4, 8, 128), BF16),
+            vmem((spans // 4, 8, 128), BF16),
+            vmem((spans // 4, 8, 128), BF16),
             vmem((3, 3, 96, 128), BF16),
             vmem((2, 96, 128), F32),
             vmem((8, 256, 128), F32),
@@ -552,6 +593,7 @@
             vmem((7, 11, 16, 256), BF16),
             vmem((5, 9, 16, 256), BF16),
             vmem((12, 11, 16, 256), BF16),
+            vmem((10, 9, 16, 256), BF16),
             vmem((12, 9, 2, 16, 256), BF16),
             vmem((12, 11, 2, 16, 256), BF16),
             vmem((12, 9, 2, 16, 256), BF16),
@@ -559,11 +601,11 @@
             vmem((16, 2, 8, 288), F32),
             vmem((4, 80, 128), F32),
             pltpu.SemaphoreType.DMA((15,)),
-            pltpu.SemaphoreType.DMA((2, 1)),
+            pltpu.SemaphoreType.DMA((2, planes // 2)),
             pltpu.SemaphoreType.DMA((2, planes // 2, heights)),
-            pltpu.SemaphoreType.DMA((2, spans)),
-            pltpu.SemaphoreType.DMA((2, 8)),
-            pltpu.SemaphoreType.DMA((2, 2, 5)),
+            pltpu.SemaphoreType.DMA((2, 2, 4)),
+            pltpu.SemaphoreType.DMA((2, 4)),
+            pltpu.SemaphoreType.DMA((2, 2, 2)),
         ]
         guess, kept, again = pl.pallas_call(
             lambda *refs: body(sizes, *refs),

time: 54.5 us -> 55.6 us (1.020)
  Pallas kernels: 50.7 us -> 51.8 us
    pallas_call x1, Pallas kernels: 50.7 us -> 51.8 us  [shards(): pl.pallas_call(lambda *refs: body(sizes, *refs), out_shape=(jax.ShapeDtyp...]
where the time goes in v4:
time: 55.6 us; the launch traced here: 55.4 us
  Pallas kernels  51.8 us (93%)
  between operations  1.93 us (3%)
  other arithmetic  1.67 us (3%)
    pallas_call x1, Pallas kernels, shards(): pl.pallas_call(lambda *refs: body(sizes, *refs), out_shape=(jax.ShapeDtyp...  51.8 us
    broadcast_in_dim x1, other arithmetic, shards(): return (guess[None].astype(BF16), (kept + again * guess)[None])  1.67 us

profile of v4, /device:TPU:1, one launch (start us, length us, event | category | flops | bytes accessed | tf_op | source)
XLA Modules:
  0.0 55.4 jit_solution(7393191801733340663)
XLA Ops:
  1.9 51.8 %denoise.1 = (f32[3,64,128]{2,1,0:T(8,128)}, f32[3,64,128]{2,1,0:T(8,128)}, f32[64,128]{1,0:T(8,128)}) custom-call(bf16[1,3,64,128]{3,2,1,0:T(8,128)(2,1)} %refs_0_.1, bf16[1,8,3,32,256]{4,3,2,1,0:T(8,128)(2,1)} %refs_1_.1, s32[1]{0:T(128)S(6)} %copy.19.refs_2_, s32[1]{0:T(128)S(6)} %copy.20.refs_3_, f32[64,256]{1,0:T(8,128)} %refs_4_.1, ...), custom_call_target="tpu_custom_call" | custom-call | tf_op jit(solution)/shard_map/denoise/pallas_call | solution.py:610
  53.7 1.7 %add_bitcast_fusion = (f32[1,3,64,128]{3,2,1,0:T(8,128)}, bf16[1,3,64,128]{3,2,1,0:T(8,128)(2,1)}) fusion(f32[3,64,128]{2,1,0:T(8,128)} %get-tuple-element.6, f32[3,64,128]{2,1,0:T(8,128)} %get-tuple-element.5, f32[64,128]{1,0:T(8,128)} %get-tuple-element.7), kind=kLoop, calls=%fused_computation | loop fusion | flops 73728 | bytes 376832 | tf_op jit(solution)/shard_map/broadcast_in_dim | solution.py:625

commit v5 on v4

--- a/solution.py
+++ b/solution.py
@@ -101,8 +101,8 @@
     slot, noisy, *weights = local
     (w_embed, w_biases, w_enter, pool_fine, pool_mid, w_squeeze, w_across) = weights[:7]
     (w_middle, rise_mid, decode_mid, rise_fine, decode_fine, w_leave) = weights[7:]
-    (send_p, got_c, planef, heightf, send_h, got_h, rowsf, send_s, got_s, send_t, got_t) = refs[:11]
-    refs = refs[11:]
+    (send_p, got_c, planef, heightf, send_h, got_h, rowsf, send_s, got_s) = refs[:9]
+    refs = refs[9:]
     (around, aroundf, entryf, tapf, tap, condf, bias, coef, bandf, w_in, w_pf, w_pm) = refs[:12]
     (w_ac, w_dm, w_df, leavef, w_lv, mask, mask2, h1, d1, d2, sq, mx, c3, v2, e2) = refs[12:27]
     (f1m, f1s, f2m, f2s, turned, outf) = refs[27:33]
@@ -132,11 +132,7 @@
     barrier = pltpu.get_barrier_semaphore()
     partners = [(mate, 0, 0), (-mate, 0, 0)]
     partners += [(2 * j, 0, k) for j in range(chips) for k in range(heights) if j or k]
-    seat = [lax.rem(s, 4), s // 4]
-    inner = [lax.rem(seat[0] + k, 4) - seat[0] for k in range(1, 4)]
-    partners += [(0, ds, 0) for ds in inner]
-    partners += [(0, 4 * k, 0) for k in range(1, spans // 4)]
-    partners += [(0, 1, 0), (0, -1, 0)]
+    partners += [(0, k, 0) for k in range(1, spans)]
     for offset in partners:
         pl.semaphore_signal(barrier, inc=1, device_id=at(*offset), device_id_type=MESH)
     def remote(src, dst, sems, index, offset):
@@ -332,43 +328,27 @@
             total = term if total is None else total + term
     rowsf[...] = total
 
-    lane = iota((8, 128), 1)
+    moved = [rowsf[0]] + [pltpu.roll(rowsf[g], 24 * g, 1) for g in range(1, 5)]
     for dest in range(spans):
-        total = jnp.zeros((8, 128), F32)
-        for g in range(5):
-            shift = (24 * g + 2 - 16 * dest) % 256
-            v = rowsf[g]
-            moved = (pltpu.roll(v, shift, 1) if shift else v)[:, 0:128]
-            total = jnp.where((lane >= 24 * g) & (lane < 24 * g + 20), moved, total)
-        send_s[dest % 4, dest // 4] = total.astype(BF16)
-
-    spot_in, four = seat
+        rel = (iota((8, 256), 1) - (16 * dest - 2)) & 255
+        total = moved[0]
+        for g in range(1, 5):
+            total = jnp.where(rel >= 24 * g, moved[g], total)
+        total = pltpu.roll(total, (2 - 16 * dest) % 256, 1)[:, 0:128]
+        send_s[dest] = total.astype(BF16)
 
     def copy_s(k):
-        src = send_s.at[lax.rem(spot_in + k, 4)]
-        return remote(src, got_s.at[spot_in], sem_s, (0, k), (0, inner[k - 1], 0))
-
-    def copy_t(k):
-        src = send_t.at[lax.rem(four + k, spans // 4)]
-        return remote(src, got_t.at[four], sem_s, (1, k), (0, 4 * k, 0))
-
-    for k in range(1, 4):
+        return remote(send_s.at[lax.rem(s + k, spans)], got_s.at[s], sem_s, (k,), (0, k, 0))
+
+    far = sorted(range(1, spans), key=lambda k: -min(k, spans - k))
+    for k in far:
         copy_s(k).start()
-    got_s[spot_in] = send_s[spot_in]
-    for k in range(1, 4):
+    got_s[s] = send_s[s]
+    for k in reversed(far):
         copy_s(k).wait_recv()
     total = got_s[0].astype(F32)
-    for k in range(1, 4):
+    for k in range(1, spans):
         total = total + got_s[k].astype(F32)
-    send_t[...] = total.astype(BF16)
-    for k in range(1, spans // 4):
-        copy_t(k).start()
-    got_t[four] = send_t[four]
-    for k in range(1, spans // 4):
-        copy_t(k).wait_recv()
-    total = got_t[0].astype(F32)
-    for k in range(1, spans // 4):
-        total = total + got_t[k].astype(F32)
     lane = iota((8, 128), 1)
     spot = lane - 24 * (lane // 24)
     outside = ((spot < 2) & (s == 0)) | ((spot >= 18) & (s == spans - 1))
@@ -532,10 +512,8 @@
         copy.wait_send()
     for j, k in rest:
         copy_h(j, k).wait_send()
-    for k in range(1, 4):
+    for k in far:
         copy_s(k).wait_send()
-    for k in range(1, spans // 4):
-        copy_t(k).wait_send()
     for g in range(2):
         copy_x(g, 1).wait_send()
         copy_x(g, -1).wait_send()
@@ -563,10 +541,8 @@
             vmem((planes // 2, heights, 5, 8, 256), BF16),
             vmem((planes // 2, heights, 5, 8, 256), BF16),
             vmem((5, 8, 256), F32),
-            vmem((4, spans // 4, 8, 128), BF16),
-            vmem((4, spans // 4, 8, 128), BF16),
-            vmem((spans // 4, 8, 128), BF16),
-            vmem((spans // 4, 8, 128), BF16),
+            vmem((spans, 8, 128), BF16),
+            vmem((spans, 8, 128), BF16),
             vmem((3, 3, 96, 128), BF16),
             vmem((2, 96, 128), F32),
             vmem((8, 256, 128), F32),
@@ -603,7 +579,7 @@
             pltpu.SemaphoreType.DMA((15,)),
             pltpu.SemaphoreType.DMA((2, planes // 2)),
             pltpu.SemaphoreType.DMA((2, planes // 2, heights)),
-            pltpu.SemaphoreType.DMA((2, 2, 4)),
+            pltpu.SemaphoreType.DMA((2, spans)),
             pltpu.SemaphoreType.DMA((2, 4)),
             pltpu.SemaphoreType.DMA((2, 2, 2)),
         ]

time: 55.6 us -> 54 us (0.971)
  Pallas kernels: 51.8 us -> 50.2 us
    pallas_call x1, Pallas kernels: 51.8 us -> 50.2 us  [shards(): pl.pallas_call(lambda *refs: body(sizes, *refs), out_shape=(jax.ShapeDtyp...]
where the time goes in v5:
time: 54 us; the launch traced here: 53.8 us
  Pallas kernels  50.2 us (93%)
  between operations  1.93 us (4%)
  other arithmetic  1.67 us (3%)
    pallas_call x1, Pallas kernels, shards(): pl.pallas_call(lambda *refs: body(sizes, *refs), out_shape=(jax.ShapeDtyp...  50.2 us
    broadcast_in_dim x1, other arithmetic, shards(): return (guess[None].astype(BF16), (kept + again * guess)[None])  1.67 us

profile of v5, /device:TPU:1, one launch (start us, length us, event | category | flops | bytes accessed | tf_op | source)
XLA Modules:
  0.0 53.8 jit_solution(7674874759478018759)
XLA Ops:
  1.9 50.2 %denoise.1 = (f32[3,64,128]{2,1,0:T(8,128)}, f32[3,64,128]{2,1,0:T(8,128)}, f32[64,128]{1,0:T(8,128)}) custom-call(bf16[1,3,64,128]{3,2,1,0:T(8,128)(2,1)} %refs_0_.1, bf16[1,8,3,32,256]{4,3,2,1,0:T(8,128)(2,1)} %refs_1_.1, s32[1]{0:T(128)S(6)} %copy.19.refs_2_, s32[1]{0:T(128)S(6)} %copy.20.refs_3_, f32[64,256]{1,0:T(8,128)} %refs_4_.1, ...), custom_call_target="tpu_custom_call" | custom-call | tf_op jit(solution)/shard_map/denoise/pallas_call | solution.py:586
  52.1 1.7 %add_bitcast_fusion = (f32[1,3,64,128]{3,2,1,0:T(8,128)}, bf16[1,3,64,128]{3,2,1,0:T(8,128)(2,1)}) fusion(f32[3,64,128]{2,1,0:T(8,128)} %get-tuple-element.6, f32[3,64,128]{2,1,0:T(8,128)} %get-tuple-element.5, f32[64,128]{1,0:T(8,128)} %get-tuple-element.7), kind=kLoop, calls=%fused_computation | loop fusion | flops 73728 | bytes 376832 | tf_op jit(solution)/shard_map/broadcast_in_dim | solution.py:601

commit v6 on v5

--- a/solution.py
+++ b/solution.py
@@ -102,7 +102,8 @@
     (w_embed, w_biases, w_enter, pool_fine, pool_mid, w_squeeze, w_across) = weights[:7]
     (w_middle, rise_mid, decode_mid, rise_fine, decode_fine, w_leave) = weights[7:]
     (send_p, got_c, planef, heightf, send_h, got_h, rowsf, send_s, got_s) = refs[:9]
-    refs = refs[9:]
+    (pick_in, pick_cell, pick_out) = refs[9:12]
+    refs = refs[12:]
     (around, aroundf, entryf, tapf, tap, condf, bias, coef, bandf, w_in, w_pf, w_pm) = refs[:12]
     (w_ac, w_dm, w_df, leavef, w_lv, mask, mask2, h1, d1, d2, sq, mx, c3, v2, e2) = refs[12:27]
     (f1m, f1s, f2m, f2s, turned, outf) = refs[27:33]
@@ -344,6 +345,24 @@
     for k in far:
         copy_s(k).start()
     got_s[s] = send_s[s]
+    line = iota((256, 160), 0)
+    channel = lax.rem(line, 8) - 3
+    m = iota((256, 160), 1)
+    rb = m // 40
+    tgt = channel * 12 + (rb * 20 + line // 8 + 7) // 8
+    pick = (channel >= 0) & (channel < 3) & (line < 176) & (m - 40 * rb == tgt)
+    pick_in[...] = onehot(pick)
+    line = iota((288, 1), 0)
+    block = lax.rem(line, 16)
+    cell = 36 * lax.rem(block, 4) + 2 * (line // 16) - 9
+    for wc in range(4):
+        tgt = (block // 4) * 32 + (cell + wc + 16) // 8
+        pick_cell[wc] = onehot(iota((288, 128), 1) == tgt)
+    lane = iota((1, 512), 1)
+    for b in (0, 1):
+        col = cell + 1 + b
+        tgt = jnp.where((col >= 0) & (col < 128), (block // 4) * 128 + col, -1)
+        pick_out[b] = onehot(lane == tgt)
     for k in reversed(far):
         copy_s(k).wait_recv()
     total = got_s[0].astype(F32)
@@ -360,22 +379,11 @@
             condf[rb * 40 + 8 * g : rb * 40 + 8 * g + 8, :] = (
                 part if rb == 0 else pltpu.roll(part, 32 * rb, 1)
             )
-    line = iota((256, 160), 0)
-    channel = lax.rem(line, 8) - 3
-    m = iota((256, 160), 1)
-    rb = m // 40
-    tgt = channel * 12 + (rb * 20 + line // 8 + 7) // 8
-    pick = (channel >= 0) & (channel < 3) & (line < 176) & (m - 40 * rb == tgt)
-    lifted = nn(onehot(pick), condf[...].astype(BF16)).astype(BF16)
-    line = iota((288, 1), 0)
-    block = lax.rem(line, 16)
-    cell = 36 * lax.rem(block, 4) + 2 * (line // 16) - 9
+    lifted = nn(pick_in[...], condf[...].astype(BF16)).astype(BF16)
     for wc in range(4):
-        tgt = (block // 4) * 32 + (cell + wc + 16) // 8
-        spot = onehot(iota((288, 128), 1) == tgt)
         lanes = slice(wc * 128, wc * 128 + 128)
         for g in range(2):
-            v = tapf[g, :, lanes] + nt(spot, lifted[48 * g : 48 * g + 128])
+            v = tapf[g, :, lanes] + nt(pick_cell[wc], lifted[48 * g : 48 * g + 128])
             tap[g, :, lanes] = v.astype(BF16)
 
     groups = ((0, 1, 2), (3, 4))
@@ -486,12 +494,7 @@
     turned[...] = out.T.reshape(16, 2, 8, 288)
     total = None
     for b in (0, 1):
-        line = iota((288, 512), 0)
-        lane = iota((288, 512), 1)
-        block = lax.rem(line, 16)
-        tgt = 36 * lax.rem(block, 4) + 2 * (line // 16) + b - 8
-        spot = onehot((block // 4 == lane // 128) & (tgt == lax.rem(lane, 128)))
-        term = nn(turned[0:10, b].reshape(80, 288).astype(BF16), spot)
+        term = nn(turned[0:10, b].reshape(80, 288).astype(BF16), pick_out[b])
         total = term if total is None else total + term
     for rb in range(4):
         outf[rb] = total[:, rb * 128 : rb * 128 + 128]
@@ -543,6 +546,9 @@
             vmem((5, 8, 256), F32),
             vmem((spans, 8, 128), BF16),
             vmem((spans, 8, 128), BF16),
+            vmem((256, 160), BF16),
+            vmem((4, 288, 128), BF16),
+            vmem((2, 288, 512), BF16),
             vmem((3, 3, 96, 128), BF16),
             vmem((2, 96, 128), F32),
             vmem((8, 256, 128), F32),

time: 54 us -> 53.7 us (level)
  no operation moved by 1% of the time
where the time goes in v6:
time: 53.7 us; the launch traced here: 53.5 us
  Pallas kernels  49.9 us (93%)
  between operations  1.93 us (4%)
  other arithmetic  1.67 us (3%)
    pallas_call x1, Pallas kernels, shards(): pl.pallas_call(lambda *refs: body(sizes, *refs), out_shape=(jax.ShapeDtyp...  49.9 us
    broadcast_in_dim x1, other arithmetic, shards(): return (guess[None].astype(BF16), (kept + again * guess)[None])  1.67 us

profile of v6, /device:TPU:1, one launch (start us, length us, event | category | flops | bytes accessed | tf_op | source)
XLA Modules:
  0.0 53.5 jit_solution(12205634136361562457)
XLA Ops:
  1.9 49.9 %denoise.1 = (f32[3,64,128]{2,1,0:T(8,128)}, f32[3,64,128]{2,1,0:T(8,128)}, f32[64,128]{1,0:T(8,128)}) custom-call(bf16[1,3,64,128]{3,2,1,0:T(8,128)(2,1)} %refs_0_.1, bf16[1,8,3,32,256]{4,3,2,1,0:T(8,128)(2,1)} %refs_1_.1, s32[1]{0:T(128)S(6)} %copy.19.refs_2_, s32[1]{0:T(128)S(6)} %copy.20.refs_3_, f32[64,256]{1,0:T(8,128)} %refs_4_.1, ...), custom_call_target="tpu_custom_call" | custom-call | tf_op jit(solution)/shard_map/denoise/pallas_call | solution.py:592
  51.9 1.7 %add_bitcast_fusion = (f32[1,3,64,128]{3,2,1,0:T(8,128)}, bf16[1,3,64,128]{3,2,1,0:T(8,128)(2,1)}) fusion(f32[3,64,128]{2,1,0:T(8,128)} %get-tuple-element.6, f32[3,64,128]{2,1,0:T(8,128)} %get-tuple-element.5, f32[64,128]{1,0:T(8,128)} %get-tuple-element.7), kind=kLoop, calls=%fused_computation | loop fusion | flops 73728 | bytes 376832 | tf_op jit(solution)/shard_map/broadcast_in_dim | solution.py:607
